TPU v7x, 256 devices: a whole 4x4x8 slice. The times are simulated.
256 devices in a mesh: dp: 8 (over x, y_lo), fsdp: 16 (over z, core), tensor: 2 (over y_hi).
Axes of the slice: x: 4, y: 4 (y_hi: 2, y_lo: 2; y = y_hi * 2 + y_lo), z: 8, core: 2. Of those that a mesh axis runs over, the one named last changes fastest.
Arguments:
- pooled: bfloat16 [8, 3072, 1152], P('dp', 'fsdp'), may hold values from -6 to 6
- ln_gain: float32 [1152], replicated, may hold values from 0.5 to 1.5
- w_in: bfloat16 [1152, 4304], P('fsdp', 'tensor'), may hold values from -0.1875 to 0.1875
- w_out: bfloat16 [4304, 1152], P('tensor', 'fsdp'), may hold values from -0.09375 to 0.09375
- texts: bfloat16 [8, 3072, 1152], P('dp', ('fsdp', 'tensor')), may hold values from -6 to 6
Outputs:
- grad_pooled: float32 [8, 3072, 1152], P('dp', 'fsdp')
- grad_in: float32 [1152, 4304], P('fsdp', 'tensor')
- grad_out: float32 [4304, 1152], P('tensor', 'fsdp')
All inputs are finite; a program needn't handle non-finite values.
Results may differ from a plain program's by a relative error of at most 0.022.
Values may be sent and summed in bfloat16 or wider, within the bound.
A program may use at most 64 MiB of HBM per device.

v0:
```python
import jax
import jax.numpy as jnp
from jax import lax
from jax.sharding import Mesh
from jax.sharding import PartitionSpec as P


ln_eps = 1e-06
norm_eps = 1e-06
logit_scale = 10.0
logit_bias = -2.0


def passed_along(block, axis, distance):
    devices = range(lax.axis_size(axis))
    route = [((i - distance) % len(devices), i) for i in devices]
    return lax.ppermute(block, axis, route)


def core_swap(block):
    return lax.ppermute(block, "core", [(0, 1), (1, 0)])


def swapped_sum(partial, axis):
    mine = partial.astype(jnp.bfloat16)
    other = lax.ppermute(mine, axis, [(0, 1), (1, 0)])
    return mine.astype(jnp.float32) + other.astype(jnp.float32)


def doubling_sum(parts, axis):
    size = lax.axis_size(axis)
    mine = [p.astype(jnp.bfloat16) for p in parts]
    totals = None
    bit = 1
    while bit < size:
        route = [(i, i ^ bit) for i in range(size)]
        others = [lax.ppermute(m, axis, route) for m in mine]
        totals = [m.astype(jnp.float32) + o.astype(jnp.float32) for m, o in zip(mine, others)]
        mine = [t.astype(jnp.bfloat16) for t in totals]
        bit *= 2
    return totals


def parity_split(values, core, chips):
    lead = values.shape[:-1]
    blocks = values.reshape(lead + (chips, 2, values.shape[-1] // (2 * chips)))
    axis = blocks.ndim - 2
    own = lax.dynamic_index_in_dim(blocks, core, axis=axis, keepdims=False)
    other = lax.dynamic_index_in_dim(blocks, 1 - core, axis=axis, keepdims=False)
    half = lead + (values.shape[-1] // 2,)
    return own.reshape(half), other.reshape(half)


def parity_join(own, other, core, chips):
    lead = own.shape[:-1]
    shape = lead + (chips, 1, own.shape[-1] // chips)
    own = own.reshape(shape)
    other = other.reshape(shape)
    even = jnp.where(core == 0, own, other)
    odd = jnp.where(core == 0, other, own)
    return jnp.concatenate([even, odd], axis=-2).reshape(lead + (2 * own.shape[-1] * chips,))


def gelu_tanh(values):
    return jax.nn.gelu(values, approximate=True)


def unit_rows(values):
    return values / jnp.sqrt(jnp.sum(values * values, axis=-1, keepdims=True) + norm_eps)


def layer(pooled, ln_gain, w_in, w_out, texts):
    rows = pooled[0].astype(jnp.float32)
    images = rows.shape[0]
    chip = lax.axis_index("z")
    chips = lax.axis_size("z")
    core = lax.axis_index("core")
    block_index = chip * 2 + core

    text_b = unit_rows(texts[0].astype(jnp.float32)).astype(jnp.bfloat16)
    block_rows = text_b.shape[0]
    offset = lax.axis_index("tensor") * block_rows
    pair = jnp.concatenate([text_b, core_swap(text_b)], axis=0)
    within = jnp.arange(block_rows, dtype=jnp.int32)

    def pair_columns(source_chip):
        first = (source_chip * 2 + core) * images + offset + within
        second = (source_chip * 2 + 1 - core) * images + offset + within
        return jnp.concatenate([first, second])

    blocks = [pair]
    sources = [chip]
    ahead = pair
    for step in range(1, chips // 2 + 1):
        ahead = passed_along(ahead, "z", 1)
        blocks.append(ahead)
        sources.append((chip - step) % chips)
    behind = pair
    for step in range(1, (chips - 1) // 2 + 1):
        behind = passed_along(behind, "z", -1)
        blocks.append(behind)
        sources.append((chip + step) % chips)
    all_texts = jnp.concatenate(blocks, axis=0)
    columns = jnp.concatenate([pair_columns(s) for s in sources], axis=0)

    stacked = jnp.stack([w_in, w_out.T])
    own_w = lax.all_gather(stacked, "z", axis=1, tiled=True)
    other_w = core_swap(own_w)
    own_in, own_out = own_w[0], own_w[1]
    other_in, other_out = other_w[0], other_w[1]

    row_mean = jnp.mean(rows, axis=1, keepdims=True)
    centred = rows - row_mean
    inv_std = lax.rsqrt(jnp.mean(centred * centred, axis=1, keepdims=True) + ln_eps)
    normal_rows = centred * inv_std
    unit_in = (normal_rows * ln_gain).astype(jnp.bfloat16)
    unit_own, unit_other = parity_split(unit_in, core, chips)
    pre_act = jnp.dot(unit_own, own_in, preferred_element_type=jnp.float32) + jnp.dot(
        unit_other, other_in, preferred_element_type=jnp.float32
    )
    hidden = gelu_tanh(pre_act).astype(jnp.bfloat16)
    mix_parts = jnp.concatenate(
        [
            jnp.einsum("rf,df->rd", hidden, own_out, preferred_element_type=jnp.float32),
            jnp.einsum("rf,df->rd", hidden, other_out, preferred_element_type=jnp.float32),
        ],
        axis=1,
    )
    mix_sum = swapped_sum(mix_parts, "tensor")
    half = mix_sum.shape[1] // 2
    mixed = rows + parity_join(mix_sum[:, :half], mix_sum[:, half:], core, chips)
    row_norm = jnp.sqrt(jnp.sum(mixed * mixed, axis=1, keepdims=True) + norm_eps)
    image_unit = mixed / row_norm
    image_b = image_unit.astype(jnp.bfloat16)
    image_places = block_index * images + jnp.arange(images, dtype=jnp.int32)

    logits = (
        logit_scale
        * jnp.einsum("rd,cd->rc", image_b, all_texts, preferred_element_type=jnp.float32)
        + logit_bias
    )
    match = (image_places[:, None] == columns[None, :]).astype(jnp.float32)
    weights = (jax.nn.sigmoid(logits) - match).astype(jnp.bfloat16)
    running = jnp.dot(weights, all_texts, preferred_element_type=jnp.float32)
    grad_unit = swapped_sum(logit_scale * running, "tensor")
    grad_mixed = (
        grad_unit - image_unit * jnp.sum(image_unit * grad_unit, axis=1, keepdims=True)
    ) / row_norm
    grad_b = grad_mixed.astype(jnp.bfloat16)
    grad_own, grad_other = parity_split(grad_b, core, chips)
    grad_hidden = jnp.einsum(
        "rd,df->rf", grad_own, own_out, preferred_element_type=jnp.float32
    ) + jnp.einsum("rd,df->rf", grad_other, other_out, preferred_element_type=jnp.float32)
    _, gelu_back = jax.vjp(gelu_tanh, pre_act)
    grad_pre = gelu_back(grad_hidden)[0].astype(jnp.bfloat16)
    unit_parts = jnp.concatenate(
        [
            jnp.einsum("rf,df->rd", grad_pre, own_in, preferred_element_type=jnp.float32),
            jnp.einsum("rf,df->rd", grad_pre, other_in, preferred_element_type=jnp.float32),
        ],
        axis=1,
    )
    unit_sum = swapped_sum(unit_parts, "tensor")
    grad_unit_in = parity_join(unit_sum[:, :half], unit_sum[:, half:], core, chips)
    scaled = grad_unit_in * ln_gain
    grad_rows = inv_std * (
        scaled
        - jnp.mean(scaled, axis=1, keepdims=True)
        - normal_rows * jnp.mean(scaled * normal_rows, axis=1, keepdims=True)
    )
    grad_pooled = (grad_mixed + grad_rows)[None]

    width = grad_pre.shape[1]
    terms_own = jnp.concatenate(
        [
            jnp.einsum("rd,rf->df", unit_own, grad_pre, preferred_element_type=jnp.float32),
            jnp.einsum("rd,rf->df", grad_own, hidden, preferred_element_type=jnp.float32),
        ],
        axis=1,
    )
    terms_other = jnp.concatenate(
        [
            jnp.einsum("rd,rf->df", unit_other, grad_pre, preferred_element_type=jnp.float32),
            jnp.einsum("rd,rf->df", grad_other, hidden, preferred_element_type=jnp.float32),
        ],
        axis=1,
    )
    terms_chip = terms_own.astype(jnp.bfloat16).astype(jnp.float32) + core_swap(
        terms_other.astype(jnp.bfloat16)
    ).astype(jnp.float32)
    terms_part = lax.psum_scatter(
        terms_chip.astype(jnp.bfloat16), "z", scatter_dimension=0, tiled=True
    )
    (total,) = doubling_sum([terms_part], "dp")
    grad_in = total[:, :width]
    grad_out = total[:, width:].T
    return (grad_pooled, grad_in, grad_out)


def solution(mesh):
    fsdp = mesh.shape["fsdp"]
    chip_mesh = Mesh(
        mesh.devices.reshape(mesh.shape["dp"], fsdp // 2, 2, mesh.shape["tensor"]),
        ("dp", "z", "core", "tensor"),
    )
    placed = (
        P("dp", ("z", "core"), None),
        P(),
        P(("z", "core"), "tensor"),
        P("tensor", ("z", "core")),
        P("dp", ("z", "core", "tensor"), None),
    )
    return jax.shard_map(
        layer,
        mesh=chip_mesh,
        in_specs=placed,
        out_specs=(
            P("dp", ("z", "core"), None),
            P(("z", "core"), "tensor"),
            P("tensor", ("z", "core")),
        ),
        check_vma=False,
    )
```

profile of v0, /device:TPU:32, one launch (start us, length us, event | category | flops | bytes accessed | tf_op | source)
XLA Modules:
  0.0 327.8 jit_solution(15502990226346934863)
XLA Ops:
  7.2 2.0 pad_maximum_fusion.3
  9.3 64.3 %all-gather.2.cloned.1.call-done = bf16[2,576,2152]{2,1,0:T(8,128)(2,1)} async-done(((bf16[2,72,2152]{2,1,0:T(8,128)(2,1)}), bf16[2,576,2152]{2,1,0:T(8,128)(2,1)}) %all-gather.2.cloned.1.call-update) | async-done | bytes 4958224 | tf_op jit(solution)/shard_map/all_gather | solution.py:107
  74.8 1.8 constant_dynamic-update-slice_fusion.8
  77.9 4.6 %collective-permute-done.2 = bf16[96,1152]{1,0:T(8,128)(2,1)S(1)} collective-permute-done((bf16[96,1152]{1,0:T(8,128)(2,1)S(1)}, bf16[96,1152]{1,0:T(8,128)(2,1)S(1)}, u32[]{:S(2)}, u32[]{:S(2)}) %collective-permute-start.2) | collective-permute-done | bytes 221216 | tf_op jit(solution)/shard_map/ppermute | solution.py:21
  83.3 1.6 collective-permute-start.3
  85.9 10.4 %collective-permute-done.3 = bf16[192,1152]{1,0:T(8,128)(2,1)} collective-permute-done((bf16[192,1152]{1,0:T(8,128)(2,1)}, bf16[192,1152]{1,0:T(8,128)(2,1)}, u32[]{:S(2)}, u32[]{:S(2)}) %collective-permute-start.3) | collective-permute-done | bytes 442400 | tf_op jit(solution)/shard_map/ppermute | solution.py:17
  96.3 1.3 collective-permute-start.4
  99.0 1.7 collective-permute-start.8
  100.7 8.5 %collective-permute-done.4 = bf16[192,1152]{1,0:T(8,128)(2,1)} collective-permute-done((bf16[192,1152]{1,0:T(8,128)(2,1)}, bf16[192,1152]{1,0:T(8,128)(2,1)}, u32[]{:S(2)}, u32[]{:S(2)}) %collective-permute-start.4) | collective-permute-done | bytes 442400 | tf_op jit(solution)/shard_map/ppermute | solution.py:17
  110.0 1.8 constant_dynamic-update-slice_fusion.6
  111.9 2.8 collective-permute-start.9
  114.7 6.4 %collective-permute-done.5 = bf16[192,1152]{1,0:T(8,128)(2,1)S(1)} collective-permute-done((bf16[192,1152]{1,0:T(8,128)(2,1)}, bf16[192,1152]{1,0:T(8,128)(2,1)S(1)}, u32[]{:S(2)}, u32[]{:S(2)}) %collective-permute-start.5) | collective-permute-done | bytes 442400 | tf_op jit(solution)/shard_map/ppermute | solution.py:17
  121.2 1.8 constant_dynamic-update-slice_fusion.5
  123.8 8.3 %collective-permute-done.6 = bf16[192,1152]{1,0:T(8,128)(2,1)S(1)} collective-permute-done((bf16[192,1152]{1,0:T(8,128)(2,1)S(1)}, bf16[192,1152]{1,0:T(8,128)(2,1)S(1)}, u32[]{:S(2)}, u32[]{:S(2)}) %collective-permute-start.6) | collective-permute-done | bytes 442400 | tf_op jit(solution)/shard_map/ppermute | solution.py:17
  132.8 1.8 constant_dynamic-update-slice_fusion.2
  135.5 4.1 %multiply_convert_fusion = (bf16[192,2152]{1,0:T(8,128)(2,1)S(1)}, f32[192,2152]{1,0:T(8,128)}) fusion(f32[192,2152]{1,0:T(8,128)S(1)} %fusion.9, bf16[192,576]{0,1:T(8,128)(2,1)S(1)} %bitcast.124, bf16[2,576,2152]{2,1,0:T(8,128)(2,1)} %collective-permute-done), kind=kOutput, calls=%fused_computation.37 | convolution fusion | flops 480119808 | bytes 6859776 | tf_op jit(solution)/shard_map/dot_general | solution.py:118
  139.7 3.0 fusion.21
  143.9 3.3 collective-permute-start.1
  148.8 5.9 %collective-permute-done.1 = bf16[192,1152]{1,0:T(8,128)(2,1)S(1)} collective-permute-done((bf16[192,1152]{1,0:T(8,128)(2,1)S(1)}, bf16[192,1152]{1,0:T(8,128)(2,1)S(1)}, u32[]{:S(2)}, u32[]{:S(2)}) %collective-permute-start.1) | collective-permute-done | bytes 442400 | tf_op jit(solution)/shard_map/ppermute | solution.py:26
  159.1 1.3 copy.19
  160.4 1.4 fusion.34
  161.7 5.3 %fusion.7 = bf16[192,1152]{1,0:T(8,128)(2,1)S(1)} fusion(bf16[1536,1152]{1,0:T(8,128)(2,1)} %constant_dynamic-update-slice_fusion, s32[1536]{0:T(1024)} %concatenate.41, s32[192]{0:T(256)} %iota_add_fusion, f32[192,1152]{1,0:T(8,128)S(1)} %copy.17, bf16[1,192,1152]{2,1,0:T(8,128)(2,1)S(1)} %copy-done, f32[192]{0:T(256)S(1)} %add_sqrt_fusion), kind=kOutput, calls=%fused_computation.21 | convolution fusion | flops 1362935808 | bytes 5316096 | tf_op jit(solution)/shard_map/dot_general | solution.py:144
  167.0 3.1 collective-permute-start.10
  170.1 6.8 %collective-permute-done.10 = bf16[192,1152]{1,0:T(8,128)(2,1)S(1)} collective-permute-done((bf16[192,1152]{1,0:T(8,128)(2,1)S(1)}, bf16[192,1152]{1,0:T(8,128)(2,1)S(1)}, u32[]{:S(2)}, u32[]{:S(2)}) %collective-permute-start.10) | collective-permute-done | bytes 442400 | tf_op jit(solution)/shard_map/ppermute | solution.py:26
  178.9 1.2 copy.20
  180.2 2.0 convolution_convert_fusion
  182.2 2.7 fusion.11
  185.0 3.5 %fusion.20 = bf16[192,2152]{1,0:T(8,128)(2,1)S(1)} fusion(f32[192,2152]{1,0:T(8,128)S(1)} %copy-done.17, f32[192,2152]{1,0:T(8,128)S(1)} %fusion.11, bf16[192,576]{0,1:T(8,128)(2,1)S(1)} %bitcast.127, bf16[2,576,2152]{2,1,0:T(8,128)(2,1)} %collective-permute-done), kind=kOutput, calls=%fused_computation.36 | convolution fusion | flops 484664832 | bytes 6859776 | tf_op jit(solution)/shard_map/rd,df->rf/dot_general | solution.py:153
  189.4 3.6 %pad_maximum_fusion = bf16[576,4304]{1,0:T(8,128)(2,1)} fusion(bf16[576,2152]{1,0:T(8,128)(2,1)S(1)} %convolution_convert_fusion, bf16[576,2152]{1,0:T(8,128)(2,1)S(1)} %convolution_convert_fusion.1), kind=kLoop, calls=%fused_computation.1 | loop fusion | flops 9916416 | bytes 9916416 | tf_op jit(solution)/shard_map/concatenate | solution.py:181
  194.6 7.0 %collective-permute-done.12 = bf16[576,4304]{1,0:T(8,128)(2,1)} collective-permute-done((bf16[576,4304]{1,0:T(8,128)(2,1)}, bf16[576,4304]{1,0:T(8,128)(2,1)}, u32[]{:S(2)}, u32[]{:S(2)}) %collective-permute-start.12) | collective-permute-done | bytes 4958240 | tf_op jit(solution)/shard_map/ppermute | solution.py:21
  201.6 7.1 %add_convert_fusion = bf16[576,4304]{1,0:T(8,128)(2,1)} fusion(bf16[576,4304]{1,0:T(8,128)(2,1)} %collective-permute-done.12, bf16[576,2152]{1,0:T(8,128)(2,1)S(1)} %convolution_convert_fusion.2, bf16[576,2152]{1,0:T(8,128)(2,1)S(1)} %convolution_convert_fusion.3), kind=kLoop, calls=%fused_computation | loop fusion | flops 17353728 | bytes 14874624 | tf_op jit(solution)/shard_map/convert_element_type | solution.py:192
  209.8 2.7 fusion.23
  212.6 2.7 fusion.24
  215.4 3.1 collective-permute-start.11
  218.5 52.7 %reduce-scatter.2.cloned.1.call-done = bf16[72,4304]{1,0:T(8,128)(2,1)} async-done(((bf16[576,4304]{1,0:T(8,128)(2,1)}), bf16[72,4304]{1,0:T(8,128)(2,1)}) %reduce-scatter.2.cloned.1.call-update) | async-done | bytes 619792 | tf_op jit(solution)/shard_map/reduce_scatter | solution.py:191
  271.2 1.5 collective-permute-start.13
  274.9 2.1 copy.21
  278.0 1.5 multiply_reduce_fusion
  279.5 1.3 copy.25
  280.7 1.3 copy.26
  282.0 5.3 %collective-permute-done.13 = bf16[72,4304]{1,0:T(8,128)(2,1)} collective-permute-done((bf16[72,4304]{1,0:T(8,128)(2,1)}, bf16[72,4304]{1,0:T(8,128)(2,1)}, u32[]{:S(2)}, u32[]{:S(2)}) %collective-permute-start.13) | collective-permute-done | bytes 619808 | tf_op jit(solution)/shard_map/ppermute | solution.py:37
  287.3 1.4 add_convert_fusion.2
  288.8 1.6 collective-permute-start.14
  290.3 1.5 fusion.37
  291.8 12.0 %collective-permute-done.14 = bf16[72,4304]{1,0:T(8,128)(2,1)S(1)} collective-permute-done((bf16[72,4304]{1,0:T(8,128)(2,1)S(1)}, bf16[72,4304]{1,0:T(8,128)(2,1)S(1)}, u32[]{:S(2)}, u32[]{:S(2)}) %collective-permute-start.14) | collective-permute-done | bytes 619808 | tf_op jit(solution)/shard_map/ppermute | solution.py:37
  304.0 3.1 collective-permute-start.15
  307.0 1.5 fusion.32
  308.5 11.1 %collective-permute-done.15 = bf16[72,4304]{1,0:T(8,128)(2,1)S(1)} collective-permute-done((bf16[72,4304]{1,0:T(8,128)(2,1)S(1)}, bf16[72,4304]{1,0:T(8,128)(2,1)S(1)}, u32[]{:S(2)}, u32[]{:S(2)}) %collective-permute-start.15) | collective-permute-done | bytes 619808 | tf_op jit(solution)/shard_map/ppermute | solution.py:37
  (108 shorter events, 26.6 us)
Async XLA Ops:
  7.2 70.5 %copy-start = (bf16[1,192,1152]{2,1,0:T(8,128)(2,1)S(1)}, bf16[1,192,1152]{2,1,0:T(8,128)(2,1)}, u32[]{:S(2)}) copy-start(bf16[1,192,1152]{2,1,0:T(8,128)(2,1)} %param.5) | copy-start | bytes 1327108
  7.2 66.5 %all-gather.2.cloned.1.call-start = ((), (), s32[]{:S(2)}) async-start(), calls=%async_computation.1 | async-start | bytes 5640192 | tf_op jit(solution)/shard_map/all_gather | solution.py:107
  9.2 88.7 %copy-start.8 = (f32[1152]{0:T(1024)S(1)}, f32[1152]{0:T(1024)}, u32[]{:S(2)}) copy-start(f32[1152]{0:T(1024)} %param.6) | copy-start | bytes 13828
  9.2 262.0 %reduce-scatter.2.cloned.1.call-start = ((), (), s32[]{:S(2)}) async-start(), calls=%async_computation.2 | async-start | bytes 5640192 | tf_op jit(solution)/shard_map/reduce_scatter | solution.py:191
  73.6 61.9 %collective-permute-start = (bf16[2,576,2152]{2,1,0:T(8,128)(2,1)}, bf16[2,576,2152]{2,1,0:T(8,128)(2,1)}, u32[]{:S(2)}, u32[]{:S(2)}) collective-permute-start(bf16[2,576,2152]{2,1,0:T(8,128)(2,1)} %all-gather.2.cloned.1.call-done), channel_id=1, source_target_pairs={{0,2},{2,0},{1,3},{3,1},{4,6},{6,4},{5,7},{7,5},{8,10},{10,8},{9,1... | collective-permute-start | bytes 14874632 | tf_op jit(solution)/shard_map/ppermute | solution.py:21
  74.7 59.9 %slice-start = ((s8[5013504]{0:T(1024)(128)(4,1)}), s8[819200]{0:T(1024)(128)(4,1)S(1)}, s32[]{:S(2)}) async-start(s8[5013504]{0:T(1024)(128)(4,1)} %bitcast.112), calls=%async_computation.3 | async-start | bytes 1638400
  76.6 5.9 %collective-permute-start.2 = (bf16[96,1152]{1,0:T(8,128)(2,1)S(1)}, bf16[96,1152]{1,0:T(8,128)(2,1)S(1)}, u32[]{:S(2)}, u32[]{:S(2)}) collective-permute-start(bf16[96,1152]{1,0:T(8,128)(2,1)S(1)} %get-tuple-element.4), channel_id=1, source_target_pairs={{0,2},{2,0},{1,3},{3,1},{4,6},{6,4},{5,7},{7,5},{8,10},{10,8},{9,1... | collective-permute-start | bytes 663560 | tf_op jit(solution)/shard_map/ppermute | solution.py:21
  77.9 21.1 %copy-start.9 = (f32[192]{0:T(256)}, f32[192]{0:T(256)S(1)}, u32[]{:S(2)}) copy-start(f32[192]{0:T(256)S(1)} %broadcast_multiply_fusion.2) | copy-start | bytes 2308
  83.3 13.0 %collective-permute-start.3 = (bf16[192,1152]{1,0:T(8,128)(2,1)}, bf16[192,1152]{1,0:T(8,128)(2,1)}, u32[]{:S(2)}, u32[]{:S(2)}) collective-permute-start(bf16[192,1152]{1,0:T(8,128)(2,1)} %pad_maximum_fusion.5), channel_id=1, source_target_pairs={{28,0},{0,4},{4,8},{8,12},{12,16},{16,20},{20,24},{24,28},{29,1},{... | collective-permute-start | bytes 1327112 | tf_op jit(solution)/shard_map/ppermute | solution.py:17
  85.1 24.9 %copy-start.13 = (f32[192]{0:T(256)}, f32[192]{0:T(256)S(1)}, u32[]{:S(2)}) copy-start(f32[192]{0:T(256)S(1)} %add_rsqrt_fusion) | copy-start | bytes 2308
  85.1 13.9 %collective-permute-start.7 = (bf16[192,1152]{1,0:T(8,128)(2,1)}, bf16[192,1152]{1,0:T(8,128)(2,1)}, u32[]{:S(2)}, u32[]{:S(2)}) collective-permute-start(bf16[192,1152]{1,0:T(8,128)(2,1)} %pad_maximum_fusion.5), channel_id=1, source_target_pairs={{4,0},{8,4},{12,8},{16,12},{20,16},{24,20},{28,24},{0,28},{5,1},{9... | collective-permute-start | bytes 1327112 | tf_op jit(solution)/shard_map/ppermute | solution.py:17
  96.3 12.9 %collective-permute-start.4 = (bf16[192,1152]{1,0:T(8,128)(2,1)}, bf16[192,1152]{1,0:T(8,128)(2,1)}, u32[]{:S(2)}, u32[]{:S(2)}) collective-permute-start(bf16[192,1152]{1,0:T(8,128)(2,1)} %collective-permute-done.3), channel_id=1, source_target_pairs={{28,0},{0,4},{4,8},{8,12},{12,16},{16,20},{20,24},{24,28},{29,1},{... | collective-permute-start | bytes 1327112 | tf_op jit(solution)/shard_map/ppermute | solution.py:17
  98.7 35.9 %slice-start.1 = ((s8[5013504]{0:T(1024)(128)(4,1)}), s8[4194304]{0:T(1024)(128)(4,1)S(1)}, s32[]{:S(2)}) async-start(s8[5013504]{0:T(1024)(128)(4,1)} %bitcast.112), calls=%async_computation.4 | async-start | bytes 8388608
  99.0 12.9 %collective-permute-start.8 = (bf16[192,1152]{1,0:T(8,128)(2,1)}, bf16[192,1152]{1,0:T(8,128)(2,1)S(1)}, u32[]{:S(2)}, u32[]{:S(2)}) collective-permute-start(bf16[192,1152]{1,0:T(8,128)(2,1)} %collective-permute-done.7), channel_id=1, source_target_pairs={{4,0},{8,4},{12,8},{16,12},{20,16},{24,20},{28,24},{0,28},{5,1},{9... | collective-permute-start | bytes 1327112 | tf_op jit(solution)/shard_map/ppermute | solution.py:17
  109.2 11.9 %collective-permute-start.5 = (bf16[192,1152]{1,0:T(8,128)(2,1)}, bf16[192,1152]{1,0:T(8,128)(2,1)S(1)}, u32[]{:S(2)}, u32[]{:S(2)}) collective-permute-start(bf16[192,1152]{1,0:T(8,128)(2,1)} %collective-permute-done.4), channel_id=1, source_target_pairs={{28,0},{0,4},{4,8},{8,12},{12,16},{16,20},{20,24},{24,28},{29,1},{... | collective-permute-start | bytes 1327112 | tf_op jit(solution)/shard_map/ppermute | solution.py:17
  111.9 36.1 %collective-permute-start.9 = (bf16[192,1152]{1,0:T(8,128)(2,1)S(1)}, bf16[192,1152]{1,0:T(8,128)(2,1)S(1)}, u32[]{:S(2)}, u32[]{:S(2)}) collective-permute-start(bf16[192,1152]{1,0:T(8,128)(2,1)S(1)} %collective-permute-done.8), channel_id=1, source_target_pairs={{4,0},{8,4},{12,8},{16,12},{20,16},{24,20},{28,24},{0,28},{5,1},{9... | collective-permute-start | bytes 1327112 | tf_op jit(solution)/shard_map/ppermute | solution.py:17
  121.1 10.9 %collective-permute-start.6 = (bf16[192,1152]{1,0:T(8,128)(2,1)S(1)}, bf16[192,1152]{1,0:T(8,128)(2,1)S(1)}, u32[]{:S(2)}, u32[]{:S(2)}) collective-permute-start(bf16[192,1152]{1,0:T(8,128)(2,1)S(1)} %collective-permute-done.5), channel_id=1, source_target_pairs={{28,0},{0,4},{4,8},{8,12},{12,16},{16,20},{20,24},{24,28},{29,1},{... | collective-permute-start | bytes 1327112 | tf_op jit(solution)/shard_map/ppermute | solution.py:17
  139.7 16.3 %copy-start.4 = (bf16[192,2152]{1,0:T(8,128)(2,1)}, bf16[192,2152]{1,0:T(8,128)(2,1)S(1)}, u32[]{:S(2)}) copy-start(bf16[192,2152]{1,0:T(8,128)(2,1)S(1)} %get-tuple-element.17) | copy-start | bytes 2479108
  143.9 10.8 %collective-permute-start.1 = (bf16[192,1152]{1,0:T(8,128)(2,1)S(1)}, bf16[192,1152]{1,0:T(8,128)(2,1)S(1)}, u32[]{:S(2)}, u32[]{:S(2)}) collective-permute-start(bf16[192,1152]{1,0:T(8,128)(2,1)S(1)} %pad_maximum_fusion.4), channel_id=1, source_target_pairs={{0,1},{1,0},{2,3},{3,2},{4,5},{5,4},{6,7},{7,6},{8,9},{9,8},{10,11... | collective-permute-start | bytes 1327112 | tf_op jit(solution)/shard_map/ppermute | solution.py:26
  161.7 15.5 %copy-start.11 = (f32[192]{0:T(256)}, f32[192]{0:T(256)S(1)}, u32[]{:S(2)}) copy-start(f32[192]{0:T(256)S(1)} %add_sqrt_fusion) | copy-start | bytes 2308
  167.0 9.9 %collective-permute-start.10 = (bf16[192,1152]{1,0:T(8,128)(2,1)S(1)}, bf16[192,1152]{1,0:T(8,128)(2,1)S(1)}, u32[]{:S(2)}, u32[]{:S(2)}) collective-permute-start(bf16[192,1152]{1,0:T(8,128)(2,1)S(1)} %fusion.7), channel_id=1, source_target_pairs={{0,1},{1,0},{2,3},{3,2},{4,5},{5,4},{6,7},{7,6},{8,9},{9,8},{10,11... | collective-permute-start | bytes 1327112 | tf_op jit(solution)/shard_map/ppermute | solution.py:26
  176.9 3.2 copy-start.1
  177.3 0.6 copy-start.15
  182.2 2.7 copy-start.17
  188.5 5.3 %copy-start.6 = (bf16[192,2152]{1,0:T(8,128)(2,1)}, bf16[192,2152]{1,0:T(8,128)(2,1)S(1)}, u32[]{:S(2)}) copy-start(bf16[192,2152]{1,0:T(8,128)(2,1)S(1)} %fusion.20) | copy-start | bytes 2479108
  189.4 3.6 %copy-start.5 = (bf16[192,2152]{1,0:T(8,128)(2,1)S(1)}, bf16[192,2152]{1,0:T(8,128)(2,1)}, u32[]{:S(2)}) copy-start(bf16[192,2152]{1,0:T(8,128)(2,1)} %copy-done.4) | copy-start | bytes 2479108
  192.9 8.7 %collective-permute-start.12 = (bf16[576,4304]{1,0:T(8,128)(2,1)}, bf16[576,4304]{1,0:T(8,128)(2,1)}, u32[]{:S(2)}, u32[]{:S(2)}) collective-permute-start(bf16[576,4304]{1,0:T(8,128)(2,1)} %pad_maximum_fusion), channel_id=1, source_target_pairs={{0,2},{2,0},{1,3},{3,1},{4,6},{6,4},{5,7},{7,5},{8,10},{10,8},{9,1... | collective-permute-start | bytes 14874632 | tf_op jit(solution)/shard_map/ppermute | solution.py:21
  208.7 1.1 copy-start.7
  215.4 57.3 %collective-permute-start.11 = (bf16[192,1152]{1,0:T(8,128)(2,1)S(1)}, bf16[192,1152]{1,0:T(8,128)(2,1)}, u32[]{:S(2)}, u32[]{:S(2)}) collective-permute-start(bf16[192,1152]{1,0:T(8,128)(2,1)S(1)} %pad_maximum_fusion.6), channel_id=1, source_target_pairs={{0,1},{1,0},{2,3},{3,2},{4,5},{5,4},{6,7},{7,6},{8,9},{9,8},{10,11... | collective-permute-start | bytes 1327112 | tf_op jit(solution)/shard_map/ppermute | solution.py:26
  271.2 16.1 %collective-permute-start.13 = (bf16[72,4304]{1,0:T(8,128)(2,1)}, bf16[72,4304]{1,0:T(8,128)(2,1)}, u32[]{:S(2)}, u32[]{:S(2)}) collective-permute-start(bf16[72,4304]{1,0:T(8,128)(2,1)} %reduce-scatter.2.cloned.1.call-done), channel_id=1, source_target_pairs={{0,32},{32,0},{64,96},{96,64},{128,160},{160,128},{192,224},{224,1... | collective-permute-start | bytes 1859336 | tf_op jit(solution)/shard_map/ppermute | solution.py:37
  279.4 10.9 %copy-start.10 = (f32[192]{0:T(256)S(1)}, f32[192]{0:T(256)}, u32[]{:S(2)}) copy-start(f32[192]{0:T(256)} %copy-done.9) | copy-start | bytes 2308
  279.5 10.9 %copy-start.14 = (f32[192]{0:T(256)S(1)}, f32[192]{0:T(256)}, u32[]{:S(2)}) copy-start(f32[192]{0:T(256)} %copy-done.13) | copy-start | bytes 2308
  282.0 25.0 %copy-start.2 = (bf16[192,1152]{1,0:T(8,128)(2,1)S(1)}, bf16[192,1152]{1,0:T(8,128)(2,1)}, u32[]{:S(2)}) copy-start(bf16[192,1152]{1,0:T(8,128)(2,1)} %copy-done.1) | copy-start | bytes 1327108
  282.0 25.0 %copy-start.3 = (f32[192,1152]{1,0:T(8,128)S(1)}, f32[192,1152]{1,0:T(8,128)}, u32[]{:S(2)}) copy-start(f32[192,1152]{1,0:T(8,128)} %copy.25) | copy-start | bytes 2654212
  282.0 25.0 %copy-start.12 = (f32[192]{0:T(256)S(1)}, f32[192]{0:T(256)}, u32[]{:S(2)}) copy-start(f32[192]{0:T(256)} %copy-done.11) | copy-start | bytes 2308
  282.0 25.0 %copy-start.16 = (f32[192]{0:T(256)S(1)}, f32[192]{0:T(256)}, u32[]{:S(2)}) copy-start(f32[192]{0:T(256)} %copy-done.15) | copy-start | bytes 2308
  288.8 15.0 %collective-permute-start.14 = (bf16[72,4304]{1,0:T(8,128)(2,1)S(1)}, bf16[72,4304]{1,0:T(8,128)(2,1)S(1)}, u32[]{:S(2)}, u32[]{:S(2)}) collective-permute-start(bf16[72,4304]{1,0:T(8,128)(2,1)S(1)} %add_convert_fusion.2), channel_id=1, source_target_pairs={{0,64},{32,96},{64,0},{96,32},{128,192},{160,224},{192,128},{224,1... | collective-permute-start | bytes 1859336 | tf_op jit(solution)/shard_map/ppermute | solution.py:37
  304.0 15.7 %collective-permute-start.15 = (bf16[72,4304]{1,0:T(8,128)(2,1)S(1)}, bf16[72,4304]{1,0:T(8,128)(2,1)S(1)}, u32[]{:S(2)}, u32[]{:S(2)}) collective-permute-start(bf16[72,4304]{1,0:T(8,128)(2,1)S(1)} %add_convert_fusion.1), channel_id=1, source_target_pairs={{0,128},{32,160},{64,192},{96,224},{128,0},{160,32},{192,64},{224,... | collective-permute-start | bytes 1859336 | tf_op jit(solution)/shard_map/ppermute | solution.py:37
Sparse Core Ops, SparseCore 0:
  10.4 63.2 all-gather.1
  208.8 62.3 reduce-scatter.1
where the time goes:
time: 331 us; the launch traced here: 328 us
  waiting for transfers between devices  203 us (61%)
  matrix products  30.6 us (9%)
  other arithmetic  30.3 us (9%)
  local copies, waits for them, and re-layouts  24.6 us (7%)
  starting transfers between devices  24.5 us (7%)
  between operations  14.5 us (4%)
    all_gather x1, waiting for transfers between devices, layer(): own_w = lax.all_gather(stacked, 'z', axis=1, tiled=True)  64.3 us
    reduce_scatter x1, waiting for transfers between devices, layer(): lax.psum_scatter(terms_chip.astype(jnp.bfloat16), 'z', scatter_dimension=...  52.7 us
    ppermute x7, waiting for transfers between devices, passed_along(): return lax.ppermute(block, axis, route)  33.6 us
    ppermute x3, waiting for transfers between devices, doubling_sum(): others = [lax.ppermute(m, axis, route) for m in mine]  28.4 us
    ppermute x3, waiting for transfers between devices, swapped_sum(): other = lax.ppermute(mine, axis, [(0, 1), (1, 0)])  12.7 us
    ppermute x3, waiting for transfers between devices, core_swap(): return lax.ppermute(block, 'core', [(0, 1), (1, 0)])  11.6 us
    unnamed x47, local copies, waits for them, and re-layouts  10.3 us
    ppermute x3, starting transfers between devices, swapped_sum(): other = lax.ppermute(mine, axis, [(0, 1), (1, 0)])  9.47 us
  transfers between devices with their start and end apart: 18, of which 13 were waited for; matrix products, arithmetic and copies ran while one was open for 13% of the time, Pallas kernels for 0%

commit v1 on v0

--- a/solution.py
+++ b/solution.py
@@ -79,29 +79,36 @@
 
     text_b = unit_rows(texts[0].astype(jnp.float32)).astype(jnp.bfloat16)
     block_rows = text_b.shape[0]
-    offset = lax.axis_index("tensor") * block_rows
-    pair = jnp.concatenate([text_b, core_swap(text_b)], axis=0)
+    half_index = lax.axis_index("tensor")
     within = jnp.arange(block_rows, dtype=jnp.int32)
 
-    def pair_columns(source_chip):
-        first = (source_chip * 2 + core) * images + offset + within
-        second = (source_chip * 2 + 1 - core) * images + offset + within
-        return jnp.concatenate([first, second])
-
-    blocks = [pair]
+    def block_columns(source_chip, parity, half):
+        return (source_chip * 2 + parity) * images + half * block_rows + within
+
+    blocks = [text_b]
     sources = [chip]
-    ahead = pair
+    ahead = text_b
     for step in range(1, chips // 2 + 1):
         ahead = passed_along(ahead, "z", 1)
         blocks.append(ahead)
         sources.append((chip - step) % chips)
-    behind = pair
+    behind = text_b
     for step in range(1, (chips - 1) // 2 + 1):
         behind = passed_along(behind, "z", -1)
         blocks.append(behind)
         sources.append((chip + step) % chips)
-    all_texts = jnp.concatenate(blocks, axis=0)
-    columns = jnp.concatenate([pair_columns(s) for s in sources], axis=0)
+    own_texts = jnp.concatenate(blocks, axis=0)
+    core_texts = jnp.concatenate([own_texts, core_swap(own_texts)], axis=0)
+    all_texts = jnp.concatenate(
+        [core_texts, lax.ppermute(core_texts, "tensor", [(0, 1), (1, 0)])], axis=0
+    )
+    columns = jnp.concatenate(
+        [block_columns(s, core, half_index) for s in sources]
+        + [block_columns(s, 1 - core, half_index) for s in sources]
+        + [block_columns(s, core, 1 - half_index) for s in sources]
+        + [block_columns(s, 1 - core, 1 - half_index) for s in sources],
+        axis=0,
+    )
 
     stacked = jnp.stack([w_in, w_out.T])
     own_w = lax.all_gather(stacked, "z", axis=1, tiled=True)
@@ -142,7 +149,7 @@
     match = (image_places[:, None] == columns[None, :]).astype(jnp.float32)
     weights = (jax.nn.sigmoid(logits) - match).astype(jnp.bfloat16)
     running = jnp.dot(weights, all_texts, preferred_element_type=jnp.float32)
-    grad_unit = swapped_sum(logit_scale * running, "tensor")
+    grad_unit = logit_scale * running
     grad_mixed = (
         grad_unit - image_unit * jnp.sum(image_unit * grad_unit, axis=1, keepdims=True)
     ) / row_norm

time: 331 us -> 354 us (1.069)
  waiting for transfers between devices: 203 us -> 231 us
  other arithmetic: 30.3 us -> 24.3 us
  matrix products: 30.6 us -> 35.5 us
    ppermute x0 -> x1, waiting for transfers between devices: none -> 65.4 us  [layer(): lax.ppermute(core_texts, 'tensor', [(0, 1), (1, 0)])]
    all_gather x1, waiting for transfers between devices: 64.3 us -> 26.5 us  [layer(): own_w = lax.all_gather(stacked, 'z', axis=1, tiled=True)]
    ppermute x3 -> x2, waiting for transfers between devices: 12.7 us -> 4.49 us  [swapped_sum(): other = lax.ppermute(mine, axis, [(0, 1), (1, 0)])]
    ppermute x3 -> x2, starting transfers between devices: 9.47 us -> 3.68 us  [swapped_sum(): other = lax.ppermute(mine, axis, [(0, 1), (1, 0)])]
    ppermute x3, waiting for transfers between devices: 28.4 us -> 33.2 us  [doubling_sum(): others = [lax.ppermute(m, axis, route) for m in mine]]
    concatenate x2 -> x3, local copies, waits for them, and re-layouts: 1.46 us -> 6.15 us  [the longest x1 4.06 us: layer(): jnp.concatenate([core_texts, lax.ppermute(core_texts, 'tensor', [(0, 1),...]
    dot_general x1, matrix products: 5.3 us -> 9.22 us  [layer(): running = jnp.dot(weights, all_texts, preferred_element_type=jnp.float32)]
    unnamed x47 -> x32, local copies, waits for them, and re-layouts: 10.3 us -> 7.76 us
  transfers between devices with their start and end apart: 18 -> 18, of which waited for: 13 -> 14; matrix products, arithmetic and copies ran while one was open for 13% -> 12% of each run, Pallas kernels for 0% -> 0%
where the time goes in v1:
time: 354 us; the launch traced here: 352 us
  waiting for transfers between devices  231 us (65%)
  matrix products  35.5 us (10%)
  other arithmetic  24.3 us (7%)
  starting transfers between devices  23.3 us (7%)
  local copies, waits for them, and re-layouts  22.8 us (6%)
  between operations  14.5 us (4%)
    ppermute x1, waiting for transfers between devices, layer(): lax.ppermute(core_texts, 'tensor', [(0, 1), (1, 0)])  65.4 us
    reduce_scatter x1, waiting for transfers between devices, layer(): lax.psum_scatter(terms_chip.astype(jnp.bfloat16), 'z', scatter_dimension=...  55.1 us
    ppermute x3, waiting for transfers between devices, doubling_sum(): others = [lax.ppermute(m, axis, route) for m in mine]  33.2 us
    ppermute x7, waiting for transfers between devices, passed_along(): return lax.ppermute(block, axis, route)  33.1 us
    all_gather x1, waiting for transfers between devices, layer(): own_w = lax.all_gather(stacked, 'z', axis=1, tiled=True)  26.5 us
    ppermute x3, waiting for transfers between devices, core_swap(): return lax.ppermute(block, 'core', [(0, 1), (1, 0)])  13.3 us
    ppermute x7, starting transfers between devices, passed_along(): return lax.ppermute(block, axis, route)  9.71 us
    dot_general x1, matrix products, layer(): running = jnp.dot(weights, all_texts, preferred_element_type=jnp.float32)  9.22 us
  transfers between devices with their start and end apart: 18, of which 14 were waited for; matrix products, arithmetic and copies ran while one was open for 12% of the time, Pallas kernels for 0%

profile of v1, /device:TPU:32, one launch (start us, length us, event | category | flops | bytes accessed | tf_op | source)
XLA Modules:
  0.0 351.5 jit_solution(8237648131272441190)
XLA Ops:
  7.2 2.0 pad_maximum_fusion.3
  9.2 1.1 fusion.38
  10.3 1.8 constant_dynamic-update-slice_fusion.16
  12.1 1.9 collective-permute-start.2
  14.8 4.4 %collective-permute-done.2 = bf16[96,1152]{1,0:T(8,128)(2,1)S(1)} collective-permute-done((bf16[96,1152]{1,0:T(8,128)(2,1)S(1)}, bf16[96,1152]{1,0:T(8,128)(2,1)S(1)}, u32[]{:S(2)}, u32[]{:S(2)}) %collective-permute-start.2) | collective-permute-done | bytes 221216 | tf_op jit(solution)/shard_map/ppermute | solution.py:17
  19.3 1.9 collective-permute-start.3
  21.2 2.3 collective-permute-start.7
  24.3 8.8 %collective-permute-done.3 = bf16[96,1152]{1,0:T(8,128)(2,1)S(1)} collective-permute-done((bf16[96,1152]{1,0:T(8,128)(2,1)S(1)}, bf16[96,1152]{1,0:T(8,128)(2,1)S(1)}, u32[]{:S(2)}, u32[]{:S(2)}) %collective-permute-start.3) | collective-permute-done | bytes 221216 | tf_op jit(solution)/shard_map/ppermute | solution.py:17
  33.1 3.5 collective-permute-start.8
  37.4 8.6 %collective-permute-done.4 = bf16[96,1152]{1,0:T(8,128)(2,1)S(1)} collective-permute-done((bf16[96,1152]{1,0:T(8,128)(2,1)S(1)}, bf16[96,1152]{1,0:T(8,128)(2,1)S(1)}, u32[]{:S(2)}, u32[]{:S(2)}) %collective-permute-start.4) | collective-permute-done | bytes 221216 | tf_op jit(solution)/shard_map/ppermute | solution.py:17
  46.9 11.2 %collective-permute-done.5 = bf16[96,1152]{1,0:T(8,128)(2,1)S(1)} collective-permute-done((bf16[96,1152]{1,0:T(8,128)(2,1)S(1)}, bf16[96,1152]{1,0:T(8,128)(2,1)S(1)}, u32[]{:S(2)}, u32[]{:S(2)}) %collective-permute-start.5) | collective-permute-done | bytes 221216 | tf_op jit(solution)/shard_map/ppermute | solution.py:17
  58.9 26.5 %all-gather.2.cloned.1.call-done = bf16[2,576,2152]{2,1,0:T(8,128)(2,1)} async-done(((bf16[2,72,2152]{2,1,0:T(8,128)(2,1)}), bf16[2,576,2152]{2,1,0:T(8,128)(2,1)}) %all-gather.2.cloned.1.call-update) | async-done | bytes 4958224 | tf_op jit(solution)/shard_map/all_gather | solution.py:114
  87.9 1.2 copy-done.8
  90.1 6.4 %collective-permute-done.9 = bf16[768,1152]{1,0:T(8,128)(2,1)S(1)} collective-permute-done((bf16[768,1152]{1,0:T(8,128)(2,1)}, bf16[768,1152]{1,0:T(8,128)(2,1)S(1)}, u32[]{:S(2)}, u32[]{:S(2)}) %collective-permute-start.9) | collective-permute-done | bytes 1769504 | tf_op jit(solution)/shard_map/ppermute | solution.py:21
  96.5 2.0 constant_dynamic-update-slice_fusion.8
  98.5 3.2 collective-permute-start.10
  102.6 2.7 fusion.8
  105.4 4.3 %multiply_convert_fusion = (bf16[192,2152]{1,0:T(8,128)(2,1)S(1)}, f32[192,2152]{1,0:T(8,128)}) fusion(f32[192,2152]{1,0:T(8,128)S(1)} %fusion.8, bf16[192,576]{0,1:T(8,128)(2,1)S(1)} %bitcast.126, bf16[2,576,2152]{2,1,0:T(8,128)(2,1)} %collective-permute-done), kind=kOutput, calls=%fused_computation.36 | convolution fusion | flops 480119808 | bytes 6859776 | tf_op jit(solution)/shard_map/dot_general | solution.py:125
  109.7 3.0 fusion.20
  112.7 1.0 fusion.21
  114.4 65.4 %collective-permute-done.10 = bf16[1536,1152]{1,0:T(8,128)(2,1)} collective-permute-done((bf16[1536,1152]{1,0:T(8,128)(2,1)}, bf16[1536,1152]{1,0:T(8,128)(2,1)}, u32[]{:S(2)}, u32[]{:S(2)}) %collective-permute-start.10) | collective-permute-done | bytes 3538976 | tf_op jit(solution)/shard_map/ppermute | solution.py:103
  179.7 4.1 %constant_dynamic-update-slice_fusion.17 = bf16[3072,1152]{1,0:T(8,128)(2,1)} fusion(bf16[3072,1152]{1,0:T(8,128)(2,1)} %get-tuple-element.6, bf16[1536,1152]{1,0:T(8,128)(2,1)} %collective-permute-done.10), kind=kLoop, calls=%fused_computation.101 | loop fusion | bytes 7077888 | tf_op jit(solution)/shard_map/concatenate | solution.py:102
  183.8 4.5 %collective-permute-done.1 = bf16[192,1152]{1,0:T(8,128)(2,1)S(1)} collective-permute-done((bf16[192,1152]{1,0:T(8,128)(2,1)S(1)}, bf16[192,1152]{1,0:T(8,128)(2,1)S(1)}, u32[]{:S(2)}, u32[]{:S(2)}) %collective-permute-start.1) | collective-permute-done | bytes 442400 | tf_op jit(solution)/shard_map/ppermute | solution.py:26
  190.2 9.2 %multiply_reduce_fusion.1 = (f32[192]{0:T(256)S(1)}, f32[192,1152]{1,0:T(8,128)S(1)}) fusion(f32[192]{0:T(256)S(1)} %add_sqrt_fusion, f32[192,1152]{1,0:T(8,128)S(1)} %copy.17, bf16[1,192,1152]{2,1,0:T(8,128)(2,1)S(1)} %copy-done, bf16[3072,1152]{1,0:T(8,128)(2,1)} %constant_dynamic-update-slice_fusion.17, s32[3072]{0:T(1024)S(1)} %concatenate.46, ...), kind=kOutput, calls=%fused_computation.69 | convolution fusion | flops 2725428992 | bytes 9304320 | tf_op jit(solution)/shard_map/dot_general | solution.py:151
  200.5 2.1 copy.20
  202.5 1.1 constant_dynamic-slice_fusion
  204.5 2.7 fusion.10
  207.2 3.6 %fusion.19 = bf16[192,2152]{1,0:T(8,128)(2,1)S(1)} fusion(f32[192,2152]{1,0:T(8,128)S(1)} %copy-done.9, f32[192,2152]{1,0:T(8,128)S(1)} %fusion.10, bf16[192,576]{0,1:T(8,128)(2,1)S(1)} %bitcast.129, bf16[2,576,2152]{2,1,0:T(8,128)(2,1)} %collective-permute-done), kind=kOutput, calls=%fused_computation.35 | convolution fusion | flops 484664832 | bytes 6859776 | tf_op jit(solution)/shard_map/rd,df->rf/dot_general | solution.py:160
  211.7 3.5 pad_maximum_fusion
  216.9 7.0 %collective-permute-done.12 = bf16[576,4304]{1,0:T(8,128)(2,1)} collective-permute-done((bf16[576,4304]{1,0:T(8,128)(2,1)}, bf16[576,4304]{1,0:T(8,128)(2,1)}, u32[]{:S(2)}, u32[]{:S(2)}) %collective-permute-start.12) | collective-permute-done | bytes 4958240 | tf_op jit(solution)/shard_map/ppermute | solution.py:21
  223.9 7.0 %add_convert_fusion = bf16[576,4304]{1,0:T(8,128)(2,1)} fusion(bf16[576,4304]{1,0:T(8,128)(2,1)} %collective-permute-done.12, bf16[576,2152]{1,0:T(8,128)(2,1)S(1)} %convolution_convert_fusion.2, bf16[576,2152]{1,0:T(8,128)(2,1)S(1)} %convolution_convert_fusion.3), kind=kLoop, calls=%fused_computation | loop fusion | flops 17353728 | bytes 14874624 | tf_op jit(solution)/shard_map/convert_element_type | solution.py:199
  230.9 2.7 fusion.23
  233.7 2.7 fusion.22
  236.5 3.3 collective-permute-start.11
  239.8 55.1 %reduce-scatter.2.cloned.1.call-done = bf16[72,4304]{1,0:T(8,128)(2,1)} async-done(((bf16[576,4304]{1,0:T(8,128)(2,1)}), bf16[72,4304]{1,0:T(8,128)(2,1)}) %reduce-scatter.2.cloned.1.call-update) | async-done | bytes 619792 | tf_op jit(solution)/shard_map/reduce_scatter | solution.py:198
  294.9 1.5 collective-permute-start.13
  297.0 1.0 copy.22
  298.0 1.3 multiply_reduce_fusion
  299.3 1.3 copy.26
  301.0 10.1 %collective-permute-done.13 = bf16[72,4304]{1,0:T(8,128)(2,1)} collective-permute-done((bf16[72,4304]{1,0:T(8,128)(2,1)}, bf16[72,4304]{1,0:T(8,128)(2,1)}, u32[]{:S(2)}, u32[]{:S(2)}) %collective-permute-start.13) | collective-permute-done | bytes 619808 | tf_op jit(solution)/shard_map/ppermute | solution.py:37
  311.0 1.4 add_convert_fusion.2
  312.5 1.6 collective-permute-start.14
  314.0 1.5 fusion.36
  315.5 12.0 %collective-permute-done.14 = bf16[72,4304]{1,0:T(8,128)(2,1)S(1)} collective-permute-done((bf16[72,4304]{1,0:T(8,128)(2,1)S(1)}, bf16[72,4304]{1,0:T(8,128)(2,1)S(1)}, u32[]{:S(2)}, u32[]{:S(2)}) %collective-permute-start.14) | collective-permute-done | bytes 619808 | tf_op jit(solution)/shard_map/ppermute | solution.py:37
  327.7 3.1 collective-permute-start.15
  330.7 1.4 fusion.31
  332.2 11.2 %collective-permute-done.15 = bf16[72,4304]{1,0:T(8,128)(2,1)S(1)} collective-permute-done((bf16[72,4304]{1,0:T(8,128)(2,1)S(1)}, bf16[72,4304]{1,0:T(8,128)(2,1)S(1)}, u32[]{:S(2)}, u32[]{:S(2)}) %collective-permute-start.15) | collective-permute-done | bytes 619808 | tf_op jit(solution)/shard_map/ppermute | solution.py:37
  343.5 1.2 slice_bitcast_fusion.22
  (100 shorter events, 16.8 us)
Async XLA Ops:
  7.2 78.3 %all-gather.2.cloned.1.call-start = ((), (), s32[]{:S(2)}) async-start(), calls=%async_computation.1 | async-start | bytes 5640192 | tf_op jit(solution)/shard_map/all_gather | solution.py:114
  9.2 285.7 %reduce-scatter.2.cloned.1.call-start = ((), (), s32[]{:S(2)}) async-start(), calls=%async_computation.2 | async-start | bytes 5640192 | tf_op jit(solution)/shard_map/reduce_scatter | solution.py:198
  12.1 7.2 %collective-permute-start.2 = (bf16[96,1152]{1,0:T(8,128)(2,1)S(1)}, bf16[96,1152]{1,0:T(8,128)(2,1)S(1)}, u32[]{:S(2)}, u32[]{:S(2)}) collective-permute-start(bf16[96,1152]{1,0:T(8,128)(2,1)S(1)} %get-tuple-element.4), channel_id=1, source_target_pairs={{28,0},{0,4},{4,8},{8,12},{12,16},{16,20},{20,24},{24,28},{29,1},{... | collective-permute-start | bytes 663560 | tf_op jit(solution)/shard_map/ppermute | solution.py:17
  14.0 7.2 %collective-permute-start.6 = (bf16[96,1152]{1,0:T(8,128)(2,1)S(1)}, bf16[96,1152]{1,0:T(8,128)(2,1)S(1)}, u32[]{:S(2)}, u32[]{:S(2)}) collective-permute-start(bf16[96,1152]{1,0:T(8,128)(2,1)S(1)} %get-tuple-element.4), channel_id=1, source_target_pairs={{4,0},{8,4},{12,8},{16,12},{20,16},{24,20},{28,24},{0,28},{5,1},{9... | collective-permute-start | bytes 663560 | tf_op jit(solution)/shard_map/ppermute | solution.py:17
  19.3 13.8 %collective-permute-start.3 = (bf16[96,1152]{1,0:T(8,128)(2,1)S(1)}, bf16[96,1152]{1,0:T(8,128)(2,1)S(1)}, u32[]{:S(2)}, u32[]{:S(2)}) collective-permute-start(bf16[96,1152]{1,0:T(8,128)(2,1)S(1)} %collective-permute-done.2), channel_id=1, source_target_pairs={{28,0},{0,4},{4,8},{8,12},{12,16},{16,20},{20,24},{24,28},{29,1},{... | collective-permute-start | bytes 663560 | tf_op jit(solution)/shard_map/ppermute | solution.py:17
  21.2 11.9 %collective-permute-start.7 = (bf16[96,1152]{1,0:T(8,128)(2,1)S(1)}, bf16[96,1152]{1,0:T(8,128)(2,1)S(1)}, u32[]{:S(2)}, u32[]{:S(2)}) collective-permute-start(bf16[96,1152]{1,0:T(8,128)(2,1)S(1)} %collective-permute-done.6), channel_id=1, source_target_pairs={{4,0},{8,4},{12,8},{16,12},{20,16},{24,20},{28,24},{0,28},{5,1},{9... | collective-permute-start | bytes 663560 | tf_op jit(solution)/shard_map/ppermute | solution.py:17
  33.1 13.0 %collective-permute-start.4 = (bf16[96,1152]{1,0:T(8,128)(2,1)S(1)}, bf16[96,1152]{1,0:T(8,128)(2,1)S(1)}, u32[]{:S(2)}, u32[]{:S(2)}) collective-permute-start(bf16[96,1152]{1,0:T(8,128)(2,1)S(1)} %collective-permute-done.3), channel_id=1, source_target_pairs={{28,0},{0,4},{4,8},{8,12},{12,16},{16,20},{20,24},{24,28},{29,1},{... | collective-permute-start | bytes 663560 | tf_op jit(solution)/shard_map/ppermute | solution.py:17
  33.1 54.0 %collective-permute-start.8 = (bf16[96,1152]{1,0:T(8,128)(2,1)S(1)}, bf16[96,1152]{1,0:T(8,128)(2,1)S(1)}, u32[]{:S(2)}, u32[]{:S(2)}) collective-permute-start(bf16[96,1152]{1,0:T(8,128)(2,1)S(1)} %collective-permute-done.7), channel_id=1, source_target_pairs={{4,0},{8,4},{12,8},{16,12},{20,16},{24,20},{28,24},{0,28},{5,1},{9... | collective-permute-start | bytes 663560 | tf_op jit(solution)/shard_map/ppermute | solution.py:17
  37.4 52.3 %copy-start.7 = (f32[1152]{0:T(1024)S(1)}, f32[1152]{0:T(1024)}, u32[]{:S(2)}) copy-start(f32[1152]{0:T(1024)} %param.6) | copy-start | bytes 13828
  37.4 52.4 %copy-start = (bf16[1,192,1152]{2,1,0:T(8,128)(2,1)S(1)}, bf16[1,192,1152]{2,1,0:T(8,128)(2,1)}, u32[]{:S(2)}) copy-start(bf16[1,192,1152]{2,1,0:T(8,128)(2,1)} %param.5) | copy-start | bytes 1327108
  46.0 12.1 %collective-permute-start.5 = (bf16[96,1152]{1,0:T(8,128)(2,1)S(1)}, bf16[96,1152]{1,0:T(8,128)(2,1)S(1)}, u32[]{:S(2)}, u32[]{:S(2)}) collective-permute-start(bf16[96,1152]{1,0:T(8,128)(2,1)S(1)} %collective-permute-done.4), channel_id=1, source_target_pairs={{28,0},{0,4},{4,8},{8,12},{12,16},{16,20},{20,24},{24,28},{29,1},{... | collective-permute-start | bytes 663560 | tf_op jit(solution)/shard_map/ppermute | solution.py:17
  85.4 19.9 %collective-permute-start = (bf16[2,576,2152]{2,1,0:T(8,128)(2,1)}, bf16[2,576,2152]{2,1,0:T(8,128)(2,1)}, u32[]{:S(2)}, u32[]{:S(2)}) collective-permute-start(bf16[2,576,2152]{2,1,0:T(8,128)(2,1)} %all-gather.2.cloned.1.call-done), channel_id=1, source_target_pairs={{0,2},{2,0},{1,3},{3,1},{4,6},{6,4},{5,7},{7,5},{8,10},{10,8},{9,1... | collective-permute-start | bytes 14874632 | tf_op jit(solution)/shard_map/ppermute | solution.py:21
  87.9 1.2 copy-start.8
  89.2 7.3 %collective-permute-start.9 = (bf16[768,1152]{1,0:T(8,128)(2,1)}, bf16[768,1152]{1,0:T(8,128)(2,1)S(1)}, u32[]{:S(2)}, u32[]{:S(2)}) collective-permute-start(bf16[768,1152]{1,0:T(8,128)(2,1)} %copy-done.8), channel_id=1, source_target_pairs={{0,2},{2,0},{1,3},{3,1},{4,6},{6,4},{5,7},{7,5},{8,10},{10,8},{9,1... | collective-permute-start | bytes 5308424 | tf_op jit(solution)/shard_map/ppermute | solution.py:21
  98.5 81.2 %collective-permute-start.10 = (bf16[1536,1152]{1,0:T(8,128)(2,1)}, bf16[1536,1152]{1,0:T(8,128)(2,1)}, u32[]{:S(2)}, u32[]{:S(2)}) collective-permute-start(bf16[1536,1152]{1,0:T(8,128)(2,1)} %get-tuple-element.5), channel_id=1, source_target_pairs={{0,1},{1,0},{2,3},{3,2},{4,5},{5,4},{6,7},{7,6},{8,9},{9,8},{10,11... | collective-permute-start | bytes 10616840 | tf_op jit(solution)/shard_map/ppermute | solution.py:103
  102.6 2.8 copy-start.5
  102.6 10.1 %slice-start = ((s8[5013504]{0:T(1024)(128)(4,1)}), s8[4194304]{0:T(1024)(128)(4,1)S(1)}, s32[]{:S(2)}) async-start(s8[5013504]{0:T(1024)(128)(4,1)} %bitcast.114), calls=%async_computation.3 | async-start | bytes 8388608
  105.4 7.4 %slice-start.1 = ((s8[5013504]{0:T(1024)(128)(4,1)}), s8[819200]{0:T(1024)(128)(4,1)S(1)}, s32[]{:S(2)}) async-start(s8[5013504]{0:T(1024)(128)(4,1)} %bitcast.114), calls=%async_computation.4 | async-start | bytes 1638400
  109.7 4.1 %copy-start.3 = (bf16[192,2152]{1,0:T(8,128)(2,1)}, bf16[192,2152]{1,0:T(8,128)(2,1)S(1)}, u32[]{:S(2)}) copy-start(bf16[192,2152]{1,0:T(8,128)(2,1)S(1)} %get-tuple-element.42) | copy-start | bytes 2479108
  113.9 74.3 %collective-permute-start.1 = (bf16[192,1152]{1,0:T(8,128)(2,1)S(1)}, bf16[192,1152]{1,0:T(8,128)(2,1)S(1)}, u32[]{:S(2)}, u32[]{:S(2)}) collective-permute-start(bf16[192,1152]{1,0:T(8,128)(2,1)S(1)} %pad_maximum_fusion.4), channel_id=1, source_target_pairs={{0,1},{1,0},{2,3},{3,2},{4,5},{5,4},{6,7},{7,6},{8,9},{9,8},{10,11... | collective-permute-start | bytes 1327112 | tf_op jit(solution)/shard_map/ppermute | solution.py:26
  199.4 3.1 copy-start.1
  199.4 4.2 %copy-start.4 = (bf16[192,2152]{1,0:T(8,128)(2,1)S(1)}, bf16[192,2152]{1,0:T(8,128)(2,1)}, u32[]{:S(2)}) copy-start(bf16[192,2152]{1,0:T(8,128)(2,1)} %copy-done.3) | copy-start | bytes 2479108
  204.5 2.7 copy-start.9
  207.2 3.6 %copy-start.6 = (bf16[192,8,1,72]{0,3,2,1:T(8,128)(2,1)S(1)}, bf16[192,8,1,72]{0,3,2,1:T(8,128)(2,1)}, u32[]{:S(2)}) copy-start(bf16[192,8,1,72]{0,3,2,1:T(8,128)(2,1)} %copy-done.5) | copy-start | bytes 663556
  215.2 8.7 %collective-permute-start.12 = (bf16[576,4304]{1,0:T(8,128)(2,1)}, bf16[576,4304]{1,0:T(8,128)(2,1)}, u32[]{:S(2)}, u32[]{:S(2)}) collective-permute-start(bf16[576,4304]{1,0:T(8,128)(2,1)} %pad_maximum_fusion), channel_id=1, source_target_pairs={{0,2},{2,0},{1,3},{3,1},{4,6},{6,4},{5,7},{7,5},{8,10},{10,8},{9,1... | collective-permute-start | bytes 14874632 | tf_op jit(solution)/shard_map/ppermute | solution.py:21
  236.5 59.9 %collective-permute-start.11 = (bf16[192,1152]{1,0:T(8,128)(2,1)S(1)}, bf16[192,1152]{1,0:T(8,128)(2,1)S(1)}, u32[]{:S(2)}, u32[]{:S(2)}) collective-permute-start(bf16[192,1152]{1,0:T(8,128)(2,1)S(1)} %pad_maximum_fusion.5), channel_id=1, source_target_pairs={{0,1},{1,0},{2,3},{3,2},{4,5},{5,4},{6,7},{7,6},{8,9},{9,8},{10,11... | collective-permute-start | bytes 1327112 | tf_op jit(solution)/shard_map/ppermute | solution.py:26
  294.9 16.1 %collective-permute-start.13 = (bf16[72,4304]{1,0:T(8,128)(2,1)}, bf16[72,4304]{1,0:T(8,128)(2,1)}, u32[]{:S(2)}, u32[]{:S(2)}) collective-permute-start(bf16[72,4304]{1,0:T(8,128)(2,1)} %reduce-scatter.2.cloned.1.call-done), channel_id=1, source_target_pairs={{0,32},{32,0},{64,96},{96,64},{128,160},{160,128},{192,224},{224,1... | collective-permute-start | bytes 1859336 | tf_op jit(solution)/shard_map/ppermute | solution.py:37
  300.9 29.8 %copy-start.2 = (f32[192,1152]{1,0:T(8,128)S(1)}, f32[192,1152]{1,0:T(8,128)}, u32[]{:S(2)}) copy-start(f32[192,1152]{1,0:T(8,128)} %copy-done.1) | copy-start | bytes 2654212
  312.5 15.0 %collective-permute-start.14 = (bf16[72,4304]{1,0:T(8,128)(2,1)S(1)}, bf16[72,4304]{1,0:T(8,128)(2,1)S(1)}, u32[]{:S(2)}, u32[]{:S(2)}) collective-permute-start(bf16[72,4304]{1,0:T(8,128)(2,1)S(1)} %add_convert_fusion.2), channel_id=1, source_target_pairs={{0,64},{32,96},{64,0},{96,32},{128,192},{160,224},{192,128},{224,1... | collective-permute-start | bytes 1859336 | tf_op jit(solution)/shard_map/ppermute | solution.py:37
  327.7 15.7 %collective-permute-start.15 = (bf16[72,4304]{1,0:T(8,128)(2,1)S(1)}, bf16[72,4304]{1,0:T(8,128)(2,1)S(1)}, u32[]{:S(2)}, u32[]{:S(2)}) collective-permute-start(bf16[72,4304]{1,0:T(8,128)(2,1)S(1)} %add_convert_fusion.1), channel_id=1, source_target_pairs={{0,128},{32,160},{64,192},{96,224},{128,0},{160,32},{192,64},{224,... | collective-permute-start | bytes 1859336 | tf_op jit(solution)/shard_map/ppermute | solution.py:37
Sparse Core Ops, SparseCore 0:
  10.3 75.0 all-gather.1
  231.1 63.8 reduce-scatter.1

commit v2 on v1

--- a/solution.py
+++ b/solution.py
@@ -99,14 +99,10 @@
         sources.append((chip + step) % chips)
     own_texts = jnp.concatenate(blocks, axis=0)
     core_texts = jnp.concatenate([own_texts, core_swap(own_texts)], axis=0)
-    all_texts = jnp.concatenate(
-        [core_texts, lax.ppermute(core_texts, "tensor", [(0, 1), (1, 0)])], axis=0
-    )
+    all_texts = core_texts
     columns = jnp.concatenate(
         [block_columns(s, core, half_index) for s in sources]
-        + [block_columns(s, 1 - core, half_index) for s in sources]
-        + [block_columns(s, core, 1 - half_index) for s in sources]
-        + [block_columns(s, 1 - core, 1 - half_index) for s in sources],
+        + [block_columns(s, 1 - core, half_index) for s in sources],
         axis=0,
     )
 
@@ -122,6 +118,7 @@
     normal_rows = centred * inv_std
     unit_in = (normal_rows * ln_gain).astype(jnp.bfloat16)
     unit_own, unit_other = parity_split(unit_in, core, chips)
+
     pre_act = jnp.dot(unit_own, own_in, preferred_element_type=jnp.float32) + jnp.dot(
         unit_other, other_in, preferred_element_type=jnp.float32
     )
@@ -149,7 +146,7 @@
     match = (image_places[:, None] == columns[None, :]).astype(jnp.float32)
     weights = (jax.nn.sigmoid(logits) - match).astype(jnp.bfloat16)
     running = jnp.dot(weights, all_texts, preferred_element_type=jnp.float32)
-    grad_unit = logit_scale * running
+    grad_unit = swapped_sum(logit_scale * running, "tensor")
     grad_mixed = (
         grad_unit - image_unit * jnp.sum(image_unit * grad_unit, axis=1, keepdims=True)
     ) / row_norm

time: 354 us -> 310 us (0.88)
  waiting for transfers between devices: 231 us -> 195 us
  matrix products: 35.5 us -> 29.5 us
    ppermute x1 -> x0, waiting for transfers between devices: 65.4 us -> none  [layer(): lax.ppermute(core_texts, 'tensor', [(0, 1), (1, 0)])]
    all_gather x1, waiting for transfers between devices: 26.5 us -> 64.3 us  [layer(): own_w = lax.all_gather(stacked, 'z', axis=1, tiled=True)]
    ppermute x7, waiting for transfers between devices: 33.1 us -> 21.2 us  [passed_along(): return lax.ppermute(block, axis, route)]
    ppermute x2 -> x3, waiting for transfers between devices: 4.49 us -> 16.2 us  [swapped_sum(): other = lax.ppermute(mine, axis, [(0, 1), (1, 0)])]
    ppermute x3, waiting for transfers between devices: 13.3 us -> 6.93 us  [core_swap(): return lax.ppermute(block, 'core', [(0, 1), (1, 0)])]
    ppermute x2 -> x3, starting transfers between devices: 3.68 us -> 9.12 us  [swapped_sum(): other = lax.ppermute(mine, axis, [(0, 1), (1, 0)])]
    dot_general x1, matrix products: 9.22 us -> 5.29 us  [layer(): running = jnp.dot(weights, all_texts, preferred_element_type=jnp.float32)]
    unnamed x32 -> x39, local copies, waits for them, and re-layouts: 7.76 us -> 7.43 us
  transfers between devices with their start and end apart: 18 -> 18, of which waited for: 14 -> 13; matrix products, arithmetic and copies ran while one was open for 12% -> 11% of each run, Pallas kernels for 0% -> 0%
where the time goes in v2:
time: 310 us; the launch traced here: 307 us
  waiting for transfers between devices  195 us (63%)
  matrix products  29.5 us (10%)
  other arithmetic  24.7 us (8%)
  starting transfers between devices  22.6 us (7%)
  local copies, waits for them, and re-layouts  21.3 us (7%)
  between operations  14.5 us (5%)
    all_gather x1, waiting for transfers between devices, layer(): own_w = lax.all_gather(stacked, 'z', axis=1, tiled=True)  64.3 us
    reduce_scatter x1, waiting for transfers between devices, layer(): lax.psum_scatter(terms_chip.astype(jnp.bfloat16), 'z', scatter_dimension=...  53.8 us
    ppermute x3, waiting for transfers between devices, doubling_sum(): others = [lax.ppermute(m, axis, route) for m in mine]  32.4 us
    ppermute x7, waiting for transfers between devices, passed_along(): return lax.ppermute(block, axis, route)  21.2 us
    ppermute x3, waiting for transfers between devices, swapped_sum(): other = lax.ppermute(mine, axis, [(0, 1), (1, 0)])  16.2 us
    ppermute x3, starting transfers between devices, swapped_sum(): other = lax.ppermute(mine, axis, [(0, 1), (1, 0)])  9.12 us
    unnamed x39, local copies, waits for them, and re-layouts  7.43 us
    ppermute x7, starting transfers between devices, passed_along(): return lax.ppermute(block, axis, route)  7.3 us
  transfers between devices with their start and end apart: 18, of which 13 were waited for; matrix products, arithmetic and copies ran while one was open for 11% of the time, Pallas kernels for 0%

profile of v2, /device:TPU:32, one launch (start us, length us, event | category | flops | bytes accessed | tf_op | source)
XLA Modules:
  0.0 307.5 jit_solution(689302460368309056)
XLA Ops:
  7.2 2.0 pad_maximum_fusion.3
  9.4 64.3 %all-gather.2.cloned.1.call-done = bf16[2,576,2152]{2,1,0:T(8,128)(2,1)} async-done(((bf16[2,72,2152]{2,1,0:T(8,128)(2,1)}), bf16[2,576,2152]{2,1,0:T(8,128)(2,1)}) %all-gather.2.cloned.1.call-update) | async-done | bytes 4958224 | tf_op jit(solution)/shard_map/all_gather | solution.py:110
  74.6 2.3 collective-permute-start.6
  78.1 4.4 %collective-permute-done.6 = bf16[96,1152]{1,0:T(8,128)(2,1)S(1)} collective-permute-done((bf16[96,1152]{1,0:T(8,128)(2,1)S(1)}, bf16[96,1152]{1,0:T(8,128)(2,1)S(1)}, u32[]{:S(2)}, u32[]{:S(2)}) %collective-permute-start.6) | collective-permute-done | bytes 221216 | tf_op jit(solution)/shard_map/ppermute | solution.py:17
  82.5 2.3 collective-permute-start.7
  85.8 4.8 %collective-permute-done.7 = bf16[96,1152]{1,0:T(8,128)(2,1)S(1)} collective-permute-done((bf16[96,1152]{1,0:T(8,128)(2,1)S(1)}, bf16[96,1152]{1,0:T(8,128)(2,1)S(1)}, u32[]{:S(2)}, u32[]{:S(2)}) %collective-permute-start.7) | collective-permute-done | bytes 221216 | tf_op jit(solution)/shard_map/ppermute | solution.py:17
  90.6 1.2 collective-permute-start.8
  94.0 5.6 %collective-permute-done.4 = bf16[96,1152]{1,0:T(8,128)(2,1)S(1)} collective-permute-done((bf16[96,1152]{1,0:T(8,128)(2,1)S(1)}, bf16[96,1152]{1,0:T(8,128)(2,1)S(1)}, u32[]{:S(2)}, u32[]{:S(2)}) %collective-permute-start.4) | collective-permute-done | bytes 221216 | tf_op jit(solution)/shard_map/ppermute | solution.py:17
  100.6 6.0 %collective-permute-done.5 = bf16[96,1152]{1,0:T(8,128)(2,1)S(1)} collective-permute-done((bf16[96,1152]{1,0:T(8,128)(2,1)S(1)}, bf16[96,1152]{1,0:T(8,128)(2,1)S(1)}, u32[]{:S(2)}, u32[]{:S(2)}) %collective-permute-start.5) | collective-permute-done | bytes 221216 | tf_op jit(solution)/shard_map/ppermute | solution.py:17
  109.4 1.9 copy-done.14
  112.2 4.1 %multiply_convert_fusion = (bf16[192,2152]{1,0:T(8,128)(2,1)S(1)}, f32[192,2152]{1,0:T(8,128)}) fusion(f32[192,2152]{1,0:T(8,128)S(1)} %fusion.9, bf16[192,576]{0,1:T(8,128)(2,1)S(1)} %bitcast.122, bf16[2,576,2152]{2,1,0:T(8,128)(2,1)} %collective-permute-done), kind=kOutput, calls=%fused_computation.37 | convolution fusion | flops 480119808 | bytes 6859776 | tf_op jit(solution)/shard_map/dot_general | solution.py:122
  116.4 3.0 fusion.21
  119.4 1.0 fusion.22
  121.4 3.0 collective-permute-start.1
  124.5 1.4 constant_dynamic-update-slice_fusion.8
  125.9 7.9 %collective-permute-done.1 = bf16[192,1152]{1,0:T(8,128)(2,1)S(1)} collective-permute-done((bf16[192,1152]{1,0:T(8,128)(2,1)}, bf16[192,1152]{1,0:T(8,128)(2,1)S(1)}, u32[]{:S(2)}, u32[]{:S(2)}) %collective-permute-start.1) | collective-permute-done | bytes 442400 | tf_op jit(solution)/shard_map/ppermute | solution.py:26
  135.2 1.3 copy.19
  136.4 1.4 fusion.34
  137.8 5.3 %fusion.7 = bf16[192,1152]{1,0:T(8,128)(2,1)S(1)} fusion(bf16[1536,1152]{1,0:T(8,128)(2,1)} %constant_dynamic-update-slice_fusion.8, s32[1536]{0:T(1024)S(1)} %concatenate.41, s32[192]{0:T(256)S(1)} %iota_add_fusion, f32[192,1152]{1,0:T(8,128)S(1)} %copy.17, bf16[1,192,1152]{2,1,0:T(8,128)(2,1)S(1)} %copy-done, f32[192]{0:T(256)S(1)} %add_sqrt_fusion), kind=kOutput, calls=%fused_computation.21 | convolution fusion | flops 1362935808 | bytes 5316096 | tf_op jit(solution)/shard_map/dot_general | solution.py:148
  143.1 3.1 %collective-permute-start.10 = (bf16[192,1152]{1,0:T(8,128)(2,1)S(1)}, bf16[192,1152]{1,0:T(8,128)(2,1)S(1)}, u32[]{:S(2)}, u32[]{:S(2)}) collective-permute-start(bf16[192,1152]{1,0:T(8,128)(2,1)S(1)} %fusion.7), channel_id=1, source_target_pairs={{0,1},{1,0},{2,3},{3,2},{4,5},{5,4},{6,7},{7,6},{8,9},{9,8},{10,11... | collective-permute-start | bytes 1327112 | tf_op jit(solution)/shard_map/ppermute | solution.py:26
  146.2 8.3 %collective-permute-done.10 = bf16[192,1152]{1,0:T(8,128)(2,1)S(1)} collective-permute-done((bf16[192,1152]{1,0:T(8,128)(2,1)S(1)}, bf16[192,1152]{1,0:T(8,128)(2,1)S(1)}, u32[]{:S(2)}, u32[]{:S(2)}) %collective-permute-start.10) | collective-permute-done | bytes 442400 | tf_op jit(solution)/shard_map/ppermute | solution.py:26
  154.9 1.1 fusion.51
  155.9 2.1 copy.20
  158.1 1.1 constant_dynamic-slice_fusion
  160.1 2.7 fusion.11
  162.8 3.6 %fusion.20 = bf16[192,2152]{1,0:T(8,128)(2,1)S(1)} fusion(f32[192,2152]{1,0:T(8,128)S(1)} %copy-done.15, f32[192,2152]{1,0:T(8,128)S(1)} %fusion.11, bf16[192,576]{0,1:T(8,128)(2,1)S(1)} %bitcast.125, bf16[2,576,2152]{2,1,0:T(8,128)(2,1)} %collective-permute-done), kind=kOutput, calls=%fused_computation.36 | convolution fusion | flops 484664832 | bytes 6859776 | tf_op jit(solution)/shard_map/rd,df->rf/dot_general | solution.py:157
  167.3 3.5 %pad_maximum_fusion = bf16[576,4304]{1,0:T(8,128)(2,1)} fusion(bf16[576,2152]{1,0:T(8,128)(2,1)S(1)} %convolution_convert_fusion, bf16[576,2152]{1,0:T(8,128)(2,1)S(1)} %convolution_convert_fusion.1), kind=kLoop, calls=%fused_computation.1 | loop fusion | flops 9916416 | bytes 9916416 | tf_op jit(solution)/shard_map/concatenate | solution.py:185
  172.6 6.9 %collective-permute-done.12 = bf16[576,4304]{1,0:T(8,128)(2,1)} collective-permute-done((bf16[576,4304]{1,0:T(8,128)(2,1)}, bf16[576,4304]{1,0:T(8,128)(2,1)}, u32[]{:S(2)}, u32[]{:S(2)}) %collective-permute-start.12) | collective-permute-done | bytes 4958240 | tf_op jit(solution)/shard_map/ppermute | solution.py:21
  179.5 7.1 %add_convert_fusion = bf16[576,4304]{1,0:T(8,128)(2,1)} fusion(bf16[576,4304]{1,0:T(8,128)(2,1)} %collective-permute-done.12, bf16[576,2152]{1,0:T(8,128)(2,1)S(1)} %convolution_convert_fusion.2, bf16[576,2152]{1,0:T(8,128)(2,1)S(1)} %convolution_convert_fusion.3), kind=kLoop, calls=%fused_computation | loop fusion | flops 17353728 | bytes 14874624 | tf_op jit(solution)/shard_map/convert_element_type | solution.py:196
  186.6 1.1 copy-done.9
  187.7 2.7 fusion.23
  190.4 2.7 fusion.24
  194.1 3.0 collective-permute-start.11
  197.1 53.8 %reduce-scatter.2.cloned.1.call-done = bf16[72,4304]{1,0:T(8,128)(2,1)} async-done(((bf16[576,4304]{1,0:T(8,128)(2,1)}), bf16[72,4304]{1,0:T(8,128)(2,1)}) %reduce-scatter.2.cloned.1.call-update) | async-done | bytes 619792 | tf_op jit(solution)/shard_map/reduce_scatter | solution.py:195
  250.9 1.5 collective-permute-start.13
  252.7 1.0 copy.21
  253.8 1.0 copy.22
  254.8 1.5 multiply_reduce_fusion
  256.3 1.3 copy.25
  257.5 1.3 copy.26
  258.8 8.2 %collective-permute-done.13 = bf16[72,4304]{1,0:T(8,128)(2,1)} collective-permute-done((bf16[72,4304]{1,0:T(8,128)(2,1)}, bf16[72,4304]{1,0:T(8,128)(2,1)}, u32[]{:S(2)}, u32[]{:S(2)}) %collective-permute-start.13) | collective-permute-done | bytes 619808 | tf_op jit(solution)/shard_map/ppermute | solution.py:37
  267.0 1.4 add_convert_fusion.2
  268.4 1.6 collective-permute-start.14
  270.3 13.1 %collective-permute-done.14 = bf16[72,4304]{1,0:T(8,128)(2,1)S(1)} collective-permute-done((bf16[72,4304]{1,0:T(8,128)(2,1)S(1)}, bf16[72,4304]{1,0:T(8,128)(2,1)S(1)}, u32[]{:S(2)}, u32[]{:S(2)}) %collective-permute-start.14) | collective-permute-done | bytes 619808 | tf_op jit(solution)/shard_map/ppermute | solution.py:37
  283.6 3.1 collective-permute-start.15
  286.7 1.5 fusion.32
  288.2 11.1 %collective-permute-done.15 = bf16[72,4304]{1,0:T(8,128)(2,1)S(1)} collective-permute-done((bf16[72,4304]{1,0:T(8,128)(2,1)S(1)}, bf16[72,4304]{1,0:T(8,128)(2,1)S(1)}, u32[]{:S(2)}, u32[]{:S(2)}) %collective-permute-start.15) | collective-permute-done | bytes 619808 | tf_op jit(solution)/shard_map/ppermute | solution.py:37
  299.4 1.2 slice_bitcast_fusion.22
  (99 shorter events, 18.1 us)
Async XLA Ops:
  7.2 66.5 %copy-start.12 = (bf16[1,96,1152]{2,1,0:T(8,128)(2,1)S(1)}, bf16[1,96,1152]{2,1,0:T(8,128)(2,1)}, u32[]{:S(2)}) copy-start(bf16[1,96,1152]{2,1,0:T(8,128)(2,1)} %param.9) | copy-start | bytes 663556
  7.2 69.7 %copy-start.13 = (f32[1152]{0:T(1024)S(1)}, f32[1152]{0:T(1024)}, u32[]{:S(2)}) copy-start(f32[1152]{0:T(1024)} %param.6) | copy-start | bytes 13828
  7.2 69.8 %copy-start = (bf16[1,192,1152]{2,1,0:T(8,128)(2,1)S(1)}, bf16[1,192,1152]{2,1,0:T(8,128)(2,1)}, u32[]{:S(2)}) copy-start(bf16[1,192,1152]{2,1,0:T(8,128)(2,1)} %param.5) | copy-start | bytes 1327108
  7.2 66.5 %all-gather.2.cloned.1.call-start = ((), (), s32[]{:S(2)}) async-start(), calls=%async_computation.1 | async-start | bytes 5640192 | tf_op jit(solution)/shard_map/all_gather | solution.py:110
  9.3 241.6 %reduce-scatter.2.cloned.1.call-start = ((), (), s32[]{:S(2)}) async-start(), calls=%async_computation.2 | async-start | bytes 5640192 | tf_op jit(solution)/shard_map/reduce_scatter | solution.py:195
  73.7 38.6 %collective-permute-start = (bf16[2,576,2152]{2,1,0:T(8,128)(2,1)}, bf16[2,576,2152]{2,1,0:T(8,128)(2,1)}, u32[]{:S(2)}, u32[]{:S(2)}) collective-permute-start(bf16[2,576,2152]{2,1,0:T(8,128)(2,1)} %all-gather.2.cloned.1.call-done), channel_id=1, source_target_pairs={{0,2},{2,0},{1,3},{3,1},{4,6},{6,4},{5,7},{7,5},{8,10},{10,8},{9,1... | collective-permute-start | bytes 14874632 | tf_op jit(solution)/shard_map/ppermute | solution.py:21
  74.6 7.8 %collective-permute-start.6 = (bf16[96,1152]{1,0:T(8,128)(2,1)S(1)}, bf16[96,1152]{1,0:T(8,128)(2,1)S(1)}, u32[]{:S(2)}, u32[]{:S(2)}) collective-permute-start(bf16[96,1152]{1,0:T(8,128)(2,1)S(1)} %get-tuple-element.4), channel_id=1, source_target_pairs={{4,0},{8,4},{12,8},{16,12},{20,16},{24,20},{28,24},{0,28},{5,1},{9... | collective-permute-start | bytes 663560 | tf_op jit(solution)/shard_map/ppermute | solution.py:17
  76.9 7.8 %collective-permute-start.2 = (bf16[96,1152]{1,0:T(8,128)(2,1)S(1)}, bf16[96,1152]{1,0:T(8,128)(2,1)S(1)}, u32[]{:S(2)}, u32[]{:S(2)}) collective-permute-start(bf16[96,1152]{1,0:T(8,128)(2,1)S(1)} %get-tuple-element.4), channel_id=1, source_target_pairs={{28,0},{0,4},{4,8},{8,12},{12,16},{16,20},{20,24},{24,28},{29,1},{... | collective-permute-start | bytes 663560 | tf_op jit(solution)/shard_map/ppermute | solution.py:17
  78.0 34.2 %copy-start.10 = (bf16[192,8,1,72]{0,3,2,1:T(8,128)(2,1)}, bf16[192,8,1,72]{0,3,2,1:T(8,128)(2,1)S(1)}, u32[]{:S(2)}) copy-start(bf16[192,8,1,72]{0,3,2,1:T(8,128)(2,1)S(1)} %get-tuple-element.15) | copy-start | bytes 663556
  78.1 33.3 %copy-start.1 = (bf16[2,576,2152]{2,1,0:T(8,128)(2,1)S(1)}, bf16[2,576,2152]{2,1,0:T(8,128)(2,1)}, u32[]{:S(2)}) copy-start(bf16[2,576,2152]{2,1,0:T(8,128)(2,1)} %all-gather.2.cloned.1.call-done) | copy-start | bytes 14874628
  82.5 8.1 %collective-permute-start.7 = (bf16[96,1152]{1,0:T(8,128)(2,1)S(1)}, bf16[96,1152]{1,0:T(8,128)(2,1)S(1)}, u32[]{:S(2)}, u32[]{:S(2)}) collective-permute-start(bf16[96,1152]{1,0:T(8,128)(2,1)S(1)} %collective-permute-done.6), channel_id=1, source_target_pairs={{4,0},{8,4},{12,8},{16,12},{20,16},{24,20},{28,24},{0,28},{5,1},{9... | collective-permute-start | bytes 663560 | tf_op jit(solution)/shard_map/ppermute | solution.py:17
  84.7 7.5 %collective-permute-start.3 = (bf16[96,1152]{1,0:T(8,128)(2,1)S(1)}, bf16[96,1152]{1,0:T(8,128)(2,1)S(1)}, u32[]{:S(2)}, u32[]{:S(2)}) collective-permute-start(bf16[96,1152]{1,0:T(8,128)(2,1)S(1)} %collective-permute-done.2), channel_id=1, source_target_pairs={{28,0},{0,4},{4,8},{8,12},{12,16},{16,20},{20,24},{24,28},{29,1},{... | collective-permute-start | bytes 663560 | tf_op jit(solution)/shard_map/ppermute | solution.py:17
  90.6 18.2 %collective-permute-start.8 = (bf16[96,1152]{1,0:T(8,128)(2,1)S(1)}, bf16[96,1152]{1,0:T(8,128)(2,1)S(1)}, u32[]{:S(2)}, u32[]{:S(2)}) collective-permute-start(bf16[96,1152]{1,0:T(8,128)(2,1)S(1)} %collective-permute-done.7), channel_id=1, source_target_pairs={{4,0},{8,4},{12,8},{16,12},{20,16},{24,20},{28,24},{0,28},{5,1},{9... | collective-permute-start | bytes 663560 | tf_op jit(solution)/shard_map/ppermute | solution.py:17
  92.3 7.3 %collective-permute-start.4 = (bf16[96,1152]{1,0:T(8,128)(2,1)S(1)}, bf16[96,1152]{1,0:T(8,128)(2,1)S(1)}, u32[]{:S(2)}, u32[]{:S(2)}) collective-permute-start(bf16[96,1152]{1,0:T(8,128)(2,1)S(1)} %collective-permute-done.3), channel_id=1, source_target_pairs={{28,0},{0,4},{4,8},{8,12},{12,16},{16,20},{20,24},{24,28},{29,1},{... | collective-permute-start | bytes 663560 | tf_op jit(solution)/shard_map/ppermute | solution.py:17
  99.6 7.0 %collective-permute-start.5 = (bf16[96,1152]{1,0:T(8,128)(2,1)S(1)}, bf16[96,1152]{1,0:T(8,128)(2,1)S(1)}, u32[]{:S(2)}, u32[]{:S(2)}) collective-permute-start(bf16[96,1152]{1,0:T(8,128)(2,1)S(1)} %collective-permute-done.4), channel_id=1, source_target_pairs={{28,0},{0,4},{4,8},{8,12},{12,16},{16,20},{20,24},{24,28},{29,1},{... | collective-permute-start | bytes 663560 | tf_op jit(solution)/shard_map/ppermute | solution.py:17
  109.4 1.9 copy-start.14
  109.4 15.0 %collective-permute-start.9 = (bf16[768,1152]{1,0:T(8,128)(2,1)}, bf16[768,1152]{1,0:T(8,128)(2,1)S(1)}, u32[]{:S(2)}, u32[]{:S(2)}) collective-permute-start(bf16[768,1152]{1,0:T(8,128)(2,1)} %get-tuple-element.17), channel_id=1, source_target_pairs={{0,2},{2,0},{1,3},{3,1},{4,6},{6,4},{5,7},{7,5},{8,10},{10,8},{9,1... | collective-permute-start | bytes 5308424 | tf_op jit(solution)/shard_map/ppermute | solution.py:21
  116.4 3.0 copy-start.6
  121.4 12.4 %collective-permute-start.1 = (bf16[192,1152]{1,0:T(8,128)(2,1)}, bf16[192,1152]{1,0:T(8,128)(2,1)S(1)}, u32[]{:S(2)}, u32[]{:S(2)}) collective-permute-start(bf16[192,1152]{1,0:T(8,128)(2,1)} %pad_maximum_fusion.4), channel_id=1, source_target_pairs={{0,1},{1,0},{2,3},{3,2},{4,5},{5,4},{6,7},{7,6},{8,9},{9,8},{10,11... | collective-permute-start | bytes 1327112 | tf_op jit(solution)/shard_map/ppermute | solution.py:26
  143.1 11.4 %collective-permute-start.10 = (bf16[192,1152]{1,0:T(8,128)(2,1)S(1)}, bf16[192,1152]{1,0:T(8,128)(2,1)S(1)}, u32[]{:S(2)}, u32[]{:S(2)}) collective-permute-start(bf16[192,1152]{1,0:T(8,128)(2,1)S(1)} %fusion.7), channel_id=1, source_target_pairs={{0,1},{1,0},{2,3},{3,2},{4,5},{5,4},{6,7},{7,6},{8,9},{9,8},{10,11... | collective-permute-start | bytes 1327112 | tf_op jit(solution)/shard_map/ppermute | solution.py:26
  154.5 1.4 copy-start.2
  155.9 3.2 %copy-start.7 = (bf16[192,2152]{1,0:T(8,128)(2,1)S(1)}, bf16[192,2152]{1,0:T(8,128)(2,1)}, u32[]{:S(2)}) copy-start(bf16[192,2152]{1,0:T(8,128)(2,1)} %copy-done.6) | copy-start | bytes 2479108
  160.1 2.7 copy-start.15
  162.8 3.6 %copy-start.11 = (bf16[192,8,1,72]{0,3,2,1:T(8,128)(2,1)S(1)}, bf16[192,8,1,72]{0,3,2,1:T(8,128)(2,1)}, u32[]{:S(2)}) copy-start(bf16[192,8,1,72]{0,3,2,1:T(8,128)(2,1)} %copy-done.10) | copy-start | bytes 663556
  166.4 5.3 %copy-start.8 = (bf16[192,2152]{1,0:T(8,128)(2,1)}, bf16[192,2152]{1,0:T(8,128)(2,1)S(1)}, u32[]{:S(2)}) copy-start(bf16[192,2152]{1,0:T(8,128)(2,1)S(1)} %fusion.20) | copy-start | bytes 2479108
  170.8 8.7 %collective-permute-start.12 = (bf16[576,4304]{1,0:T(8,128)(2,1)}, bf16[576,4304]{1,0:T(8,128)(2,1)}, u32[]{:S(2)}, u32[]{:S(2)}) collective-permute-start(bf16[576,4304]{1,0:T(8,128)(2,1)} %pad_maximum_fusion), channel_id=1, source_target_pairs={{0,2},{2,0},{1,3},{3,1},{4,6},{6,4},{5,7},{7,5},{8,10},{10,8},{9,1... | collective-permute-start | bytes 14874632 | tf_op jit(solution)/shard_map/ppermute | solution.py:21
  186.6 1.1 copy-start.9
  194.1 58.3 %collective-permute-start.11 = (bf16[192,1152]{1,0:T(8,128)(2,1)}, bf16[192,1152]{1,0:T(8,128)(2,1)S(1)}, u32[]{:S(2)}, u32[]{:S(2)}) collective-permute-start(bf16[192,1152]{1,0:T(8,128)(2,1)} %pad_maximum_fusion.5), channel_id=1, source_target_pairs={{0,1},{1,0},{2,3},{3,2},{4,5},{5,4},{6,7},{7,6},{8,9},{9,8},{10,11... | collective-permute-start | bytes 1327112 | tf_op jit(solution)/shard_map/ppermute | solution.py:26
  250.9 16.1 %collective-permute-start.13 = (bf16[72,4304]{1,0:T(8,128)(2,1)}, bf16[72,4304]{1,0:T(8,128)(2,1)}, u32[]{:S(2)}, u32[]{:S(2)}) collective-permute-start(bf16[72,4304]{1,0:T(8,128)(2,1)} %reduce-scatter.2.cloned.1.call-done), channel_id=1, source_target_pairs={{0,32},{32,0},{64,96},{96,64},{128,160},{160,128},{192,224},{224,1... | collective-permute-start | bytes 1859336 | tf_op jit(solution)/shard_map/ppermute | solution.py:37
  258.8 11.2 %copy-start.5 = (f32[1,192,1152]{2,1,0:T(8,128)S(1)}, f32[1,192,1152]{2,1,0:T(8,128)}, u32[]{:S(2)}) copy-start(f32[1,192,1152]{2,1,0:T(8,128)} %copy.26) | copy-start | bytes 2654212
  268.4 18.3 %copy-start.3 = (bf16[192,1152]{1,0:T(8,128)(2,1)S(1)}, bf16[192,1152]{1,0:T(8,128)(2,1)}, u32[]{:S(2)}) copy-start(bf16[192,1152]{1,0:T(8,128)(2,1)} %copy-done.2) | copy-start | bytes 1327108
  268.4 18.3 %copy-start.4 = (f32[192,1152]{1,0:T(8,128)S(1)}, f32[192,1152]{1,0:T(8,128)}, u32[]{:S(2)}) copy-start(f32[192,1152]{1,0:T(8,128)} %copy.25) | copy-start | bytes 2654212
  268.4 15.0 %collective-permute-start.14 = (bf16[72,4304]{1,0:T(8,128)(2,1)S(1)}, bf16[72,4304]{1,0:T(8,128)(2,1)S(1)}, u32[]{:S(2)}, u32[]{:S(2)}) collective-permute-start(bf16[72,4304]{1,0:T(8,128)(2,1)S(1)} %add_convert_fusion.2), channel_id=1, source_target_pairs={{0,64},{32,96},{64,0},{96,32},{128,192},{160,224},{192,128},{224,1... | collective-permute-start | bytes 1859336 | tf_op jit(solution)/shard_map/ppermute | solution.py:37
  283.6 15.7 %collective-permute-start.15 = (bf16[72,4304]{1,0:T(8,128)(2,1)S(1)}, bf16[72,4304]{1,0:T(8,128)(2,1)S(1)}, u32[]{:S(2)}, u32[]{:S(2)}) collective-permute-start(bf16[72,4304]{1,0:T(8,128)(2,1)S(1)} %add_convert_fusion.1), channel_id=1, source_target_pairs={{0,128},{32,160},{64,192},{96,224},{128,0},{160,32},{192,64},{224,... | collective-permute-start | bytes 1859336 | tf_op jit(solution)/shard_map/ppermute | solution.py:37
Sparse Core Ops, SparseCore 0:
  10.4 63.2 all-gather.1
  186.7 64.1 reduce-scatter.1

commit v3 on v2

--- a/solution.py
+++ b/solution.py
@@ -27,18 +27,27 @@
     return mine.astype(jnp.float32) + other.astype(jnp.float32)
 
 
-def doubling_sum(parts, axis):
-    size = lax.axis_size(axis)
-    mine = [p.astype(jnp.bfloat16) for p in parts]
-    totals = None
-    bit = 1
-    while bit < size:
-        route = [(i, i ^ bit) for i in range(size)]
-        others = [lax.ppermute(m, axis, route) for m in mine]
-        totals = [m.astype(jnp.float32) + o.astype(jnp.float32) for m, o in zip(mine, others)]
-        mine = [t.astype(jnp.bfloat16) for t in totals]
-        bit *= 2
-    return totals
+def ring_dp_sum(values):
+    size = lax.axis_size("dp")
+    pair = [(i, i ^ 1) for i in range(size)]
+    mine = values.astype(jnp.bfloat16)
+    paired = (
+        mine.astype(jnp.float32) + lax.ppermute(mine, "dp", pair).astype(jnp.float32)
+    ).astype(jnp.bfloat16)
+    left = lax.ppermute(paired, "dp", [(i, (i + 2) % size) for i in range(size)])
+    right = lax.ppermute(paired, "dp", [(i, (i - 2) % size) for i in range(size)])
+    across = lax.ppermute(right, "dp", [(i, (i - 2) % size) for i in range(size)])
+    ring = size // 2
+    place = lax.axis_index("dp") // 2
+    by_offset = [paired, right, across, left]
+    slots = []
+    for p in range(ring):
+        offset = (p - place) % ring
+        value = by_offset[0]
+        for k in range(1, ring):
+            value = jnp.where(offset == k, by_offset[k], value)
+        slots.append(value.astype(jnp.float32))
+    return (slots[0] + slots[1]) + (slots[2] + slots[3])
 
 
 def parity_split(values, core, chips):
@@ -118,7 +127,6 @@
     normal_rows = centred * inv_std
     unit_in = (normal_rows * ln_gain).astype(jnp.bfloat16)
     unit_own, unit_other = parity_split(unit_in, core, chips)
-
     pre_act = jnp.dot(unit_own, own_in, preferred_element_type=jnp.float32) + jnp.dot(
         unit_other, other_in, preferred_element_type=jnp.float32
     )
@@ -195,7 +203,7 @@
     terms_part = lax.psum_scatter(
         terms_chip.astype(jnp.bfloat16), "z", scatter_dimension=0, tiled=True
     )
-    (total,) = doubling_sum([terms_part], "dp")
+    total = ring_dp_sum(terms_part)
     grad_in = total[:, :width]
     grad_out = total[:, width:].T
     return (grad_pooled, grad_in, grad_out)

time: 310 us -> 311 us (level)
  waiting for transfers between devices: 195 us -> 191 us
    ppermute x3 -> x4, waiting for transfers between devices: 32.4 us -> 29.6 us  [the longest x1 10.8 us: ring_dp_sum(): lax.ppermute(paired, 'dp', [(i, (i - 2) % size) for i in range(size)])]
    ppermute x3 -> x4, starting transfers between devices: 6.1 us -> 8 us  [the longest x1 3.69 us: ring_dp_sum(): lax.ppermute(right, 'dp', [(i, (i - 2) % size) for i in range(size)])]
    unnamed x39 -> x55, local copies, waits for them, and re-layouts: 7.43 us -> 7.43 us
  transfers between devices with their start and end apart: 18 -> 19, of which waited for: 13 -> 13; matrix products, arithmetic and copies ran while one was open for 11% -> 12% of each run, Pallas kernels for 0% -> 0%
where the time goes in v3:
time: 311 us; the launch traced here: 307 us
  waiting for transfers between devices  191 us (61%)
  matrix products  29.6 us (10%)
  starting transfers between devices  24.9 us (8%)
  other arithmetic  24.9 us (8%)
  local copies, waits for them, and re-layouts  21.9 us (7%)
  between operations  14.5 us (5%)
    all_gather x1, waiting for transfers between devices, layer(): own_w = lax.all_gather(stacked, 'z', axis=1, tiled=True)  64.3 us
    reduce_scatter x1, waiting for transfers between devices, layer(): lax.psum_scatter(terms_chip.astype(jnp.bfloat16), 'z', scatter_dimension=...  54.5 us
    ppermute x7, waiting for transfers between devices, passed_along(): return lax.ppermute(block, axis, route)  21.2 us
    ppermute x3, waiting for transfers between devices, swapped_sum(): other = lax.ppermute(mine, axis, [(0, 1), (1, 0)])  14.6 us
    ppermute x1, waiting for transfers between devices, ring_dp_sum(): lax.ppermute(paired, 'dp', [(i, (i - 2) % size) for i in range(size)])  10.8 us
    ppermute x1, waiting for transfers between devices, ring_dp_sum(): lax.ppermute(right, 'dp', [(i, (i - 2) % size) for i in range(size)])  10.1 us
    ppermute x3, starting transfers between devices, swapped_sum(): other = lax.ppermute(mine, axis, [(0, 1), (1, 0)])  9.48 us
    ppermute x1, waiting for transfers between devices, ring_dp_sum(): lax.ppermute(mine, 'dp', pair).astype(jnp.float32)  8.59 us
  transfers between devices with their start and end apart: 19, of which 13 were waited for; matrix products, arithmetic and copies ran while one was open for 12% of the time, Pallas kernels for 0%

profile of v3, /device:TPU:32, one launch (start us, length us, event | category | flops | bytes accessed | tf_op | source)
XLA Modules:
  0.0 306.9 jit_solution(12865408686497047200)
XLA Ops:
  7.2 2.0 pad_maximum_fusion.3
  9.4 64.3 %all-gather.2.cloned.1.call-done = bf16[2,576,2152]{2,1,0:T(8,128)(2,1)} async-done(((bf16[2,72,2152]{2,1,0:T(8,128)(2,1)}), bf16[2,576,2152]{2,1,0:T(8,128)(2,1)}) %all-gather.2.cloned.1.call-update) | async-done | bytes 4958224 | tf_op jit(solution)/shard_map/all_gather | solution.py:119
  74.6 2.3 collective-permute-start.6
  78.1 4.4 %collective-permute-done.6 = bf16[96,1152]{1,0:T(8,128)(2,1)S(1)} collective-permute-done((bf16[96,1152]{1,0:T(8,128)(2,1)S(1)}, bf16[96,1152]{1,0:T(8,128)(2,1)S(1)}, u32[]{:S(2)}, u32[]{:S(2)}) %collective-permute-start.6) | collective-permute-done | bytes 221216 | tf_op jit(solution)/shard_map/ppermute | solution.py:17
  82.5 2.3 collective-permute-start.7
  85.8 4.8 %collective-permute-done.7 = bf16[96,1152]{1,0:T(8,128)(2,1)S(1)} collective-permute-done((bf16[96,1152]{1,0:T(8,128)(2,1)S(1)}, bf16[96,1152]{1,0:T(8,128)(2,1)S(1)}, u32[]{:S(2)}, u32[]{:S(2)}) %collective-permute-start.7) | collective-permute-done | bytes 221216 | tf_op jit(solution)/shard_map/ppermute | solution.py:17
  90.6 1.2 collective-permute-start.8
  94.0 5.6 %collective-permute-done.4 = bf16[96,1152]{1,0:T(8,128)(2,1)S(1)} collective-permute-done((bf16[96,1152]{1,0:T(8,128)(2,1)S(1)}, bf16[96,1152]{1,0:T(8,128)(2,1)S(1)}, u32[]{:S(2)}, u32[]{:S(2)}) %collective-permute-start.4) | collective-permute-done | bytes 221216 | tf_op jit(solution)/shard_map/ppermute | solution.py:17
  100.6 6.0 %collective-permute-done.5 = bf16[96,1152]{1,0:T(8,128)(2,1)S(1)} collective-permute-done((bf16[96,1152]{1,0:T(8,128)(2,1)S(1)}, bf16[96,1152]{1,0:T(8,128)(2,1)S(1)}, u32[]{:S(2)}, u32[]{:S(2)}) %collective-permute-start.5) | collective-permute-done | bytes 221216 | tf_op jit(solution)/shard_map/ppermute | solution.py:17
  109.5 1.8 copy-done.19
  112.2 4.2 %multiply_convert_fusion = (bf16[192,2152]{1,0:T(8,128)(2,1)S(1)}, f32[192,2152]{1,0:T(8,128)}) fusion(f32[192,2152]{1,0:T(8,128)S(1)} %fusion.9, bf16[192,576]{0,1:T(8,128)(2,1)S(1)} %bitcast.122, bf16[2,576,2152]{2,1,0:T(8,128)(2,1)} %collective-permute-done), kind=kOutput, calls=%fused_computation.37 | convolution fusion | flops 480119808 | bytes 6859776 | tf_op jit(solution)/shard_map/dot_general | solution.py:130
  116.4 3.0 fusion.21
  119.4 1.0 fusion.22
  120.6 3.3 %collective-permute-start.1 = (bf16[192,1152]{1,0:T(8,128)(2,1)S(1)}, bf16[192,1152]{1,0:T(8,128)(2,1)S(1)}, u32[]{:S(2)}, u32[]{:S(2)}) collective-permute-start(bf16[192,1152]{1,0:T(8,128)(2,1)S(1)} %pad_maximum_fusion.4), channel_id=1, source_target_pairs={{0,1},{1,0},{2,3},{3,2},{4,5},{5,4},{6,7},{7,6},{8,9},{9,8},{10,11... | collective-permute-start | bytes 1327112 | tf_op jit(solution)/shard_map/ppermute | solution.py:26
  124.0 2.9 constant_dynamic-update-slice_fusion.8
  126.9 6.2 %collective-permute-done.1 = bf16[192,1152]{1,0:T(8,128)(2,1)S(1)} collective-permute-done((bf16[192,1152]{1,0:T(8,128)(2,1)S(1)}, bf16[192,1152]{1,0:T(8,128)(2,1)S(1)}, u32[]{:S(2)}, u32[]{:S(2)}) %collective-permute-start.1) | collective-permute-done | bytes 442400 | tf_op jit(solution)/shard_map/ppermute | solution.py:26
  134.5 1.3 copy.19
  135.8 1.4 fusion.34
  137.2 5.3 %fusion.7 = bf16[192,1152]{1,0:T(8,128)(2,1)S(1)} fusion(bf16[1536,1152]{1,0:T(8,128)(2,1)} %constant_dynamic-update-slice_fusion.8, s32[1536]{0:T(1024)S(1)} %concatenate.41, s32[192]{0:T(256)S(1)} %iota_add_fusion, f32[192,1152]{1,0:T(8,128)S(1)} %copy.17, bf16[1,192,1152]{2,1,0:T(8,128)(2,1)S(1)} %copy-done, f32[192]{0:T(256)S(1)} %add_sqrt_fusion), kind=kOutput, calls=%fused_computation.21 | convolution fusion | flops 1362935808 | bytes 5316096 | tf_op jit(solution)/shard_map/dot_general | solution.py:156
  142.5 3.1 %collective-permute-start.10 = (bf16[192,1152]{1,0:T(8,128)(2,1)S(1)}, bf16[192,1152]{1,0:T(8,128)(2,1)S(1)}, u32[]{:S(2)}, u32[]{:S(2)}) collective-permute-start(bf16[192,1152]{1,0:T(8,128)(2,1)S(1)} %fusion.7), channel_id=1, source_target_pairs={{0,1},{1,0},{2,3},{3,2},{4,5},{5,4},{6,7},{7,6},{8,9},{9,8},{10,11... | collective-permute-start | bytes 1327112 | tf_op jit(solution)/shard_map/ppermute | solution.py:26
  145.6 8.4 %collective-permute-done.10 = bf16[192,1152]{1,0:T(8,128)(2,1)S(1)} collective-permute-done((bf16[192,1152]{1,0:T(8,128)(2,1)S(1)}, bf16[192,1152]{1,0:T(8,128)(2,1)S(1)}, u32[]{:S(2)}, u32[]{:S(2)}) %collective-permute-start.10) | collective-permute-done | bytes 442400 | tf_op jit(solution)/shard_map/ppermute | solution.py:26
  154.3 1.1 fusion.51
  155.3 2.1 copy.20
  157.5 1.1 constant_dynamic-slice_fusion
  159.5 2.7 fusion.11
  162.2 3.6 %fusion.20 = bf16[192,2152]{1,0:T(8,128)(2,1)S(1)} fusion(f32[192,2152]{1,0:T(8,128)S(1)} %copy-done.23, f32[192,2152]{1,0:T(8,128)S(1)} %fusion.11, bf16[192,576]{0,1:T(8,128)(2,1)S(1)} %bitcast.125, bf16[2,576,2152]{2,1,0:T(8,128)(2,1)} %collective-permute-done), kind=kOutput, calls=%fused_computation.36 | convolution fusion | flops 484664832 | bytes 6859776 | tf_op jit(solution)/shard_map/rd,df->rf/dot_general | solution.py:165
  166.7 3.5 %pad_maximum_fusion = bf16[576,4304]{1,0:T(8,128)(2,1)} fusion(bf16[576,2152]{1,0:T(8,128)(2,1)S(1)} %convolution_convert_fusion, bf16[576,2152]{1,0:T(8,128)(2,1)S(1)} %convolution_convert_fusion.1), kind=kLoop, calls=%fused_computation.1 | loop fusion | flops 9916416 | bytes 9916416 | tf_op jit(solution)/shard_map/concatenate | solution.py:193
  171.9 6.9 %collective-permute-done.12 = bf16[576,4304]{1,0:T(8,128)(2,1)} collective-permute-done((bf16[576,4304]{1,0:T(8,128)(2,1)}, bf16[576,4304]{1,0:T(8,128)(2,1)}, u32[]{:S(2)}, u32[]{:S(2)}) %collective-permute-start.12) | collective-permute-done | bytes 4958240 | tf_op jit(solution)/shard_map/ppermute | solution.py:21
  178.9 7.1 %add_convert_fusion = bf16[576,4304]{1,0:T(8,128)(2,1)} fusion(bf16[576,4304]{1,0:T(8,128)(2,1)} %collective-permute-done.12, bf16[576,2152]{1,0:T(8,128)(2,1)S(1)} %convolution_convert_fusion.2, bf16[576,2152]{1,0:T(8,128)(2,1)S(1)} %convolution_convert_fusion.3), kind=kLoop, calls=%fused_computation | loop fusion | flops 17353728 | bytes 14874624 | tf_op jit(solution)/shard_map/convert_element_type | solution.py:204
  186.0 1.1 copy-done.8
  187.1 2.7 fusion.23
  189.8 2.7 fusion.24
  192.7 3.1 %collective-permute-start.11 = (bf16[192,1152]{1,0:T(8,128)(2,1)S(1)}, bf16[192,1152]{1,0:T(8,128)(2,1)S(1)}, u32[]{:S(2)}, u32[]{:S(2)}) collective-permute-start(bf16[192,1152]{1,0:T(8,128)(2,1)S(1)} %pad_maximum_fusion.5), channel_id=1, source_target_pairs={{0,1},{1,0},{2,3},{3,2},{4,5},{5,4},{6,7},{7,6},{8,9},{9,8},{10,11... | collective-permute-start | bytes 1327112 | tf_op jit(solution)/shard_map/ppermute | solution.py:26
  195.8 54.5 %reduce-scatter.2.cloned.1.call-done = bf16[72,4304]{1,0:T(8,128)(2,1)} async-done(((bf16[576,4304]{1,0:T(8,128)(2,1)}), bf16[72,4304]{1,0:T(8,128)(2,1)}) %reduce-scatter.2.cloned.1.call-update) | async-done | bytes 619792 | tf_op jit(solution)/shard_map/reduce_scatter | solution.py:203
  250.3 1.5 collective-permute-start.13
  252.3 1.0 copy.22
  253.4 1.9 multiply_reduce_fusion
  255.2 1.3 copy.25
  256.5 1.3 copy.26
  257.8 8.6 %collective-permute-done.13 = bf16[72,4304]{1,0:T(8,128)(2,1)} collective-permute-done((bf16[72,4304]{1,0:T(8,128)(2,1)}, bf16[72,4304]{1,0:T(8,128)(2,1)}, u32[]{:S(2)}, u32[]{:S(2)}) %collective-permute-start.13) | collective-permute-done | bytes 619808 | tf_op jit(solution)/shard_map/ppermute | solution.py:35
  266.4 1.4 add_convert_fusion.1
  267.8 2.8 collective-permute-start.15
  270.6 1.5 fusion.37
  272.2 10.8 %collective-permute-done.15 = bf16[72,4304]{1,0:T(8,128)(2,1)S(1)} collective-permute-done((bf16[72,4304]{1,0:T(8,128)(2,1)S(1)}, bf16[72,4304]{1,0:T(8,128)(2,1)S(1)}, u32[]{:S(2)}, u32[]{:S(2)}) %collective-permute-start.15) | collective-permute-done | bytes 619808 | tf_op jit(solution)/shard_map/ppermute | solution.py:38
  283.0 3.7 %collective-permute-start.16 = (bf16[72,4304]{1,0:T(8,128)(2,1)S(1)}, bf16[72,4304]{1,0:T(8,128)(2,1)S(1)}, u32[]{:S(2)}, u32[]{:S(2)}) collective-permute-start(bf16[72,4304]{1,0:T(8,128)(2,1)S(1)} %collective-permute-done.15), channel_id=1, source_target_pairs={{0,192},{32,224},{64,0},{96,32},{128,64},{160,96},{192,128},{224,1... | collective-permute-start | bytes 1859336 | tf_op jit(solution)/shard_map/ppermute | solution.py:39
  286.7 1.5 fusion.32
  288.2 10.1 %collective-permute-done.16 = bf16[72,4304]{1,0:T(8,128)(2,1)S(1)} collective-permute-done((bf16[72,4304]{1,0:T(8,128)(2,1)S(1)}, bf16[72,4304]{1,0:T(8,128)(2,1)S(1)}, u32[]{:S(2)}, u32[]{:S(2)}) %collective-permute-start.16) | collective-permute-done | bytes 619808 | tf_op jit(solution)/shard_map/ppermute | solution.py:39
  298.8 1.2 slice_bitcast_fusion.22
  (116 shorter events, 16.8 us)
Async XLA Ops:
  7.2 66.5 %copy-start.11 = (bf16[1,96,1152]{2,1,0:T(8,128)(2,1)S(1)}, bf16[1,96,1152]{2,1,0:T(8,128)(2,1)}, u32[]{:S(2)}) copy-start(bf16[1,96,1152]{2,1,0:T(8,128)(2,1)} %param.9) | copy-start | bytes 663556
  7.2 69.7 %copy-start.12 = (f32[1152]{0:T(1024)S(1)}, f32[1152]{0:T(1024)}, u32[]{:S(2)}) copy-start(f32[1152]{0:T(1024)} %param.6) | copy-start | bytes 13828
  7.2 69.8 %copy-start = (bf16[1,192,1152]{2,1,0:T(8,128)(2,1)S(1)}, bf16[1,192,1152]{2,1,0:T(8,128)(2,1)}, u32[]{:S(2)}) copy-start(bf16[1,192,1152]{2,1,0:T(8,128)(2,1)} %param.5) | copy-start | bytes 1327108
  7.2 66.5 %all-gather.2.cloned.1.call-start = ((), (), s32[]{:S(2)}) async-start(), calls=%async_computation.1 | async-start | bytes 5640192 | tf_op jit(solution)/shard_map/all_gather | solution.py:119
  9.3 241.0 %reduce-scatter.2.cloned.1.call-start = ((), (), s32[]{:S(2)}) async-start(), calls=%async_computation.2 | async-start | bytes 5640192 | tf_op jit(solution)/shard_map/reduce_scatter | solution.py:203
  73.7 38.5 %collective-permute-start = (bf16[2,576,2152]{2,1,0:T(8,128)(2,1)}, bf16[2,576,2152]{2,1,0:T(8,128)(2,1)}, u32[]{:S(2)}, u32[]{:S(2)}) collective-permute-start(bf16[2,576,2152]{2,1,0:T(8,128)(2,1)} %all-gather.2.cloned.1.call-done), channel_id=1, source_target_pairs={{0,2},{2,0},{1,3},{3,1},{4,6},{6,4},{5,7},{7,5},{8,10},{10,8},{9,1... | collective-permute-start | bytes 14874632 | tf_op jit(solution)/shard_map/ppermute | solution.py:21
  74.6 7.8 %collective-permute-start.6 = (bf16[96,1152]{1,0:T(8,128)(2,1)S(1)}, bf16[96,1152]{1,0:T(8,128)(2,1)S(1)}, u32[]{:S(2)}, u32[]{:S(2)}) collective-permute-start(bf16[96,1152]{1,0:T(8,128)(2,1)S(1)} %get-tuple-element.4), channel_id=1, source_target_pairs={{4,0},{8,4},{12,8},{16,12},{20,16},{24,20},{28,24},{0,28},{5,1},{9... | collective-permute-start | bytes 663560 | tf_op jit(solution)/shard_map/ppermute | solution.py:17
  76.9 7.8 %collective-permute-start.2 = (bf16[96,1152]{1,0:T(8,128)(2,1)S(1)}, bf16[96,1152]{1,0:T(8,128)(2,1)S(1)}, u32[]{:S(2)}, u32[]{:S(2)}) collective-permute-start(bf16[96,1152]{1,0:T(8,128)(2,1)S(1)} %get-tuple-element.4), channel_id=1, source_target_pairs={{28,0},{0,4},{4,8},{8,12},{12,16},{16,20},{20,24},{24,28},{29,1},{... | collective-permute-start | bytes 663560 | tf_op jit(solution)/shard_map/ppermute | solution.py:17
  77.5 0.6 copy-start.13
  77.7 8.0 %copy-start.17 = (f32[192]{0:T(256)}, f32[192]{0:T(256)S(1)}, u32[]{:S(2)}) copy-start(f32[192]{0:T(256)S(1)} %add_rsqrt_fusion) | copy-start | bytes 2308
  78.0 34.2 %copy-start.9 = (bf16[192,8,1,72]{0,3,2,1:T(8,128)(2,1)}, bf16[192,8,1,72]{0,3,2,1:T(8,128)(2,1)S(1)}, u32[]{:S(2)}) copy-start(bf16[192,8,1,72]{0,3,2,1:T(8,128)(2,1)S(1)} %get-tuple-element.15) | copy-start | bytes 663556
  78.1 33.2 %copy-start.1 = (bf16[2,576,2152]{2,1,0:T(8,128)(2,1)S(1)}, bf16[2,576,2152]{2,1,0:T(8,128)(2,1)}, u32[]{:S(2)}) copy-start(bf16[2,576,2152]{2,1,0:T(8,128)(2,1)} %all-gather.2.cloned.1.call-done) | copy-start | bytes 14874628
  82.5 8.1 %collective-permute-start.7 = (bf16[96,1152]{1,0:T(8,128)(2,1)S(1)}, bf16[96,1152]{1,0:T(8,128)(2,1)S(1)}, u32[]{:S(2)}, u32[]{:S(2)}) collective-permute-start(bf16[96,1152]{1,0:T(8,128)(2,1)S(1)} %collective-permute-done.6), channel_id=1, source_target_pairs={{4,0},{8,4},{12,8},{16,12},{20,16},{24,20},{28,24},{0,28},{5,1},{9... | collective-permute-start | bytes 663560 | tf_op jit(solution)/shard_map/ppermute | solution.py:17
  84.7 7.5 %collective-permute-start.3 = (bf16[96,1152]{1,0:T(8,128)(2,1)S(1)}, bf16[96,1152]{1,0:T(8,128)(2,1)S(1)}, u32[]{:S(2)}, u32[]{:S(2)}) collective-permute-start(bf16[96,1152]{1,0:T(8,128)(2,1)S(1)} %collective-permute-done.2), channel_id=1, source_target_pairs={{28,0},{0,4},{4,8},{8,12},{12,16},{16,20},{20,24},{24,28},{29,1},{... | collective-permute-start | bytes 663560 | tf_op jit(solution)/shard_map/ppermute | solution.py:17
  90.6 18.2 %collective-permute-start.8 = (bf16[96,1152]{1,0:T(8,128)(2,1)S(1)}, bf16[96,1152]{1,0:T(8,128)(2,1)S(1)}, u32[]{:S(2)}, u32[]{:S(2)}) collective-permute-start(bf16[96,1152]{1,0:T(8,128)(2,1)S(1)} %collective-permute-done.7), channel_id=1, source_target_pairs={{4,0},{8,4},{12,8},{16,12},{20,16},{24,20},{28,24},{0,28},{5,1},{9... | collective-permute-start | bytes 663560 | tf_op jit(solution)/shard_map/ppermute | solution.py:17
  92.3 7.3 %collective-permute-start.4 = (bf16[96,1152]{1,0:T(8,128)(2,1)S(1)}, bf16[96,1152]{1,0:T(8,128)(2,1)S(1)}, u32[]{:S(2)}, u32[]{:S(2)}) collective-permute-start(bf16[96,1152]{1,0:T(8,128)(2,1)S(1)} %collective-permute-done.3), channel_id=1, source_target_pairs={{28,0},{0,4},{4,8},{8,12},{12,16},{16,20},{20,24},{24,28},{29,1},{... | collective-permute-start | bytes 663560 | tf_op jit(solution)/shard_map/ppermute | solution.py:17
  99.6 7.0 %collective-permute-start.5 = (bf16[96,1152]{1,0:T(8,128)(2,1)S(1)}, bf16[96,1152]{1,0:T(8,128)(2,1)S(1)}, u32[]{:S(2)}, u32[]{:S(2)}) collective-permute-start(bf16[96,1152]{1,0:T(8,128)(2,1)S(1)} %collective-permute-done.4), channel_id=1, source_target_pairs={{28,0},{0,4},{4,8},{8,12},{12,16},{16,20},{20,24},{24,28},{29,1},{... | collective-permute-start | bytes 663560 | tf_op jit(solution)/shard_map/ppermute | solution.py:17
  109.4 1.9 copy-start.19
  109.4 14.6 %collective-permute-start.9 = (bf16[768,1152]{1,0:T(8,128)(2,1)}, bf16[768,1152]{1,0:T(8,128)(2,1)}, u32[]{:S(2)}, u32[]{:S(2)}) collective-permute-start(bf16[768,1152]{1,0:T(8,128)(2,1)} %get-tuple-element.17), channel_id=1, source_target_pairs={{0,2},{2,0},{1,3},{3,1},{4,6},{6,4},{5,7},{7,5},{8,10},{10,8},{9,1... | collective-permute-start | bytes 5308424 | tf_op jit(solution)/shard_map/ppermute | solution.py:21
  116.4 3.0 copy-start.5
  120.6 12.5 %collective-permute-start.1 = (bf16[192,1152]{1,0:T(8,128)(2,1)S(1)}, bf16[192,1152]{1,0:T(8,128)(2,1)S(1)}, u32[]{:S(2)}, u32[]{:S(2)}) collective-permute-start(bf16[192,1152]{1,0:T(8,128)(2,1)S(1)} %pad_maximum_fusion.4), channel_id=1, source_target_pairs={{0,1},{1,0},{2,3},{3,2},{4,5},{5,4},{6,7},{7,6},{8,9},{9,8},{10,11... | collective-permute-start | bytes 1327112 | tf_op jit(solution)/shard_map/ppermute | solution.py:26
  137.2 17.1 %copy-start.15 = (f32[192]{0:T(256)}, f32[192]{0:T(256)S(1)}, u32[]{:S(2)}) copy-start(f32[192]{0:T(256)S(1)} %add_sqrt_fusion) | copy-start | bytes 2308
  142.5 11.5 %collective-permute-start.10 = (bf16[192,1152]{1,0:T(8,128)(2,1)S(1)}, bf16[192,1152]{1,0:T(8,128)(2,1)S(1)}, u32[]{:S(2)}, u32[]{:S(2)}) collective-permute-start(bf16[192,1152]{1,0:T(8,128)(2,1)S(1)} %fusion.7), channel_id=1, source_target_pairs={{0,1},{1,0},{2,3},{3,2},{4,5},{5,4},{6,7},{7,6},{8,9},{9,8},{10,11... | collective-permute-start | bytes 1327112 | tf_op jit(solution)/shard_map/ppermute | solution.py:26
  153.9 1.4 copy-start.2
  154.3 3.2 %copy-start.20 = (f32[192]{0:T(256)}, f32[192]{0:T(256)S(1)}, u32[]{:S(2)}) copy-start(f32[192]{0:T(256)S(1)} %multiply_reduce_fusion.1) | copy-start | bytes 2308
  155.3 3.2 %copy-start.6 = (bf16[192,2152]{1,0:T(8,128)(2,1)S(1)}, bf16[192,2152]{1,0:T(8,128)(2,1)}, u32[]{:S(2)}) copy-start(bf16[192,2152]{1,0:T(8,128)(2,1)} %copy-done.5) | copy-start | bytes 2479108
  159.5 2.7 copy-start.23
  162.2 3.6 %copy-start.10 = (bf16[192,8,1,72]{0,3,2,1:T(8,128)(2,1)S(1)}, bf16[192,8,1,72]{0,3,2,1:T(8,128)(2,1)}, u32[]{:S(2)}) copy-start(bf16[192,8,1,72]{0,3,2,1:T(8,128)(2,1)} %copy-done.9) | copy-start | bytes 663556
  165.8 5.3 %copy-start.7 = (bf16[192,2152]{1,0:T(8,128)(2,1)}, bf16[192,2152]{1,0:T(8,128)(2,1)S(1)}, u32[]{:S(2)}) copy-start(bf16[192,2152]{1,0:T(8,128)(2,1)S(1)} %fusion.20) | copy-start | bytes 2479108
  170.2 8.7 %collective-permute-start.12 = (bf16[576,4304]{1,0:T(8,128)(2,1)}, bf16[576,4304]{1,0:T(8,128)(2,1)}, u32[]{:S(2)}, u32[]{:S(2)}) collective-permute-start(bf16[576,4304]{1,0:T(8,128)(2,1)} %pad_maximum_fusion), channel_id=1, source_target_pairs={{0,2},{2,0},{1,3},{3,1},{4,6},{6,4},{5,7},{7,5},{8,10},{10,8},{9,1... | collective-permute-start | bytes 14874632 | tf_op jit(solution)/shard_map/ppermute | solution.py:21
  185.9 1.1 copy-start.8
  192.7 59.1 %collective-permute-start.11 = (bf16[192,1152]{1,0:T(8,128)(2,1)S(1)}, bf16[192,1152]{1,0:T(8,128)(2,1)S(1)}, u32[]{:S(2)}, u32[]{:S(2)}) collective-permute-start(bf16[192,1152]{1,0:T(8,128)(2,1)S(1)} %pad_maximum_fusion.5), channel_id=1, source_target_pairs={{0,1},{1,0},{2,3},{3,2},{4,5},{5,4},{6,7},{7,6},{8,9},{9,8},{10,11... | collective-permute-start | bytes 1327112 | tf_op jit(solution)/shard_map/ppermute | solution.py:26
  250.3 16.1 %collective-permute-start.13 = (bf16[72,4304]{1,0:T(8,128)(2,1)}, bf16[72,4304]{1,0:T(8,128)(2,1)}, u32[]{:S(2)}, u32[]{:S(2)}) collective-permute-start(bf16[72,4304]{1,0:T(8,128)(2,1)} %reduce-scatter.2.cloned.1.call-done), channel_id=1, source_target_pairs={{0,32},{32,0},{64,96},{96,64},{128,160},{160,128},{192,224},{224,1... | collective-permute-start | bytes 1859336 | tf_op jit(solution)/shard_map/ppermute | solution.py:35
  256.5 14.1 %copy-start.14 = (f32[192]{0:T(256)S(1)}, f32[192]{0:T(256)}, u32[]{:S(2)}) copy-start(f32[192]{0:T(256)} %copy-done.13) | copy-start | bytes 2308
  256.5 14.1 %copy-start.18 = (f32[192]{0:T(256)S(1)}, f32[192]{0:T(256)}, u32[]{:S(2)}) copy-start(f32[192]{0:T(256)} %copy-done.17) | copy-start | bytes 2308
  257.8 14.3 %copy-start.22 = (f32[192]{0:T(256)S(1)}, f32[192]{0:T(256)}, u32[]{:S(2)}) copy-start(f32[192]{0:T(256)} %get-tuple-element.7) | copy-start | bytes 2308
  257.8 28.9 %copy-start.3 = (bf16[192,1152]{1,0:T(8,128)(2,1)S(1)}, bf16[192,1152]{1,0:T(8,128)(2,1)}, u32[]{:S(2)}) copy-start(bf16[192,1152]{1,0:T(8,128)(2,1)} %copy-done.2) | copy-start | bytes 1327108
  257.8 28.9 %copy-start.4 = (f32[192,1152]{1,0:T(8,128)S(1)}, f32[192,1152]{1,0:T(8,128)}, u32[]{:S(2)}) copy-start(f32[192,1152]{1,0:T(8,128)} %copy.25) | copy-start | bytes 2654212
  257.8 28.9 %copy-start.16 = (f32[192]{0:T(256)S(1)}, f32[192]{0:T(256)}, u32[]{:S(2)}) copy-start(f32[192]{0:T(256)} %copy-done.15) | copy-start | bytes 2308
  257.8 28.9 %copy-start.21 = (f32[192]{0:T(256)S(1)}, f32[192]{0:T(256)}, u32[]{:S(2)}) copy-start(f32[192]{0:T(256)} %copy-done.20) | copy-start | bytes 2308
  267.8 15.2 %collective-permute-start.15 = (bf16[72,4304]{1,0:T(8,128)(2,1)S(1)}, bf16[72,4304]{1,0:T(8,128)(2,1)S(1)}, u32[]{:S(2)}, u32[]{:S(2)}) collective-permute-start(bf16[72,4304]{1,0:T(8,128)(2,1)S(1)} %add_convert_fusion.1), channel_id=1, source_target_pairs={{0,192},{32,224},{64,0},{96,32},{128,64},{160,96},{192,128},{224,1... | collective-permute-start | bytes 1859336 | tf_op jit(solution)/shard_map/ppermute | solution.py:38
  272.1 16.1 %collective-permute-start.14 = (bf16[72,4304]{1,0:T(8,128)(2,1)S(1)}, bf16[72,4304]{1,0:T(8,128)(2,1)S(1)}, u32[]{:S(2)}, u32[]{:S(2)}) collective-permute-start(bf16[72,4304]{1,0:T(8,128)(2,1)S(1)} %add_convert_fusion.1), channel_id=1, source_target_pairs={{0,64},{32,96},{64,128},{96,160},{128,192},{160,224},{192,0},{224,... | collective-permute-start | bytes 1859336 | tf_op jit(solution)/shard_map/ppermute | solution.py:37
  283.0 15.3 %collective-permute-start.16 = (bf16[72,4304]{1,0:T(8,128)(2,1)S(1)}, bf16[72,4304]{1,0:T(8,128)(2,1)S(1)}, u32[]{:S(2)}, u32[]{:S(2)}) collective-permute-start(bf16[72,4304]{1,0:T(8,128)(2,1)S(1)} %collective-permute-done.15), channel_id=1, source_target_pairs={{0,192},{32,224},{64,0},{96,32},{128,64},{160,96},{192,128},{224,1... | collective-permute-start | bytes 1859336 | tf_op jit(solution)/shard_map/ppermute | solution.py:39
Sparse Core Ops, SparseCore 0:
  10.4 63.2 all-gather.1
  186.1 64.1 reduce-scatter.1

commit v4 on v2

--- a/solution.py
+++ b/solution.py
@@ -23,7 +23,13 @@
 
 def swapped_sum(partial, axis):
     mine = partial.astype(jnp.bfloat16)
-    other = lax.ppermute(mine, axis, [(0, 1), (1, 0)])
+    half = mine.shape[0] // 2
+    other = jnp.concatenate(
+        [
+            lax.ppermute(mine[:half], axis, [(0, 1), (1, 0)]),
+            lax.ppermute(mine[half:], axis, [(0, 1), (1, 0)]),
+        ]
+    )
     return mine.astype(jnp.float32) + other.astype(jnp.float32)
 
 
@@ -118,7 +124,6 @@
     normal_rows = centred * inv_std
     unit_in = (normal_rows * ln_gain).astype(jnp.bfloat16)
     unit_own, unit_other = parity_split(unit_in, core, chips)
-
     pre_act = jnp.dot(unit_own, own_in, preferred_element_type=jnp.float32) + jnp.dot(
         unit_other, other_in, preferred_element_type=jnp.float32
     )

time: 310 us -> 313 us (level)
  waiting for transfers between devices: 195 us -> 202 us
  local copies, waits for them, and re-layouts: 21.3 us -> 14.8 us
    ppermute x3, waiting for transfers between devices: 32.4 us -> 37 us  [doubling_sum(): others = [lax.ppermute(m, axis, route) for m in mine]]
    ppermute x3 -> x6, waiting for transfers between devices: 16.2 us -> 18.9 us  [the longest x3 11.1 us: swapped_sum(): lax.ppermute(mine[:half], axis, [(0, 1), (1, 0)])]
    ppermute x3 -> x6, starting transfers between devices: 9.12 us -> 11 us  [the longest x3 9.47 us: swapped_sum(): lax.ppermute(mine[:half], axis, [(0, 1), (1, 0)])]
    unnamed x39 -> x27, local copies, waits for them, and re-layouts: 7.43 us -> 6.42 us
  transfers between devices with their start and end apart: 18 -> 21, of which waited for: 13 -> 15; matrix products, arithmetic and copies ran while one was open for 11% -> 10% of each run, Pallas kernels for 0% -> 0%
where the time goes in v4:
time: 313 us; the launch traced here: 310 us
  waiting for transfers between devices  202 us (65%)
  matrix products  31.4 us (10%)
  starting transfers between devices  24.7 us (8%)
  other arithmetic  22.6 us (7%)
  local copies, waits for them, and re-layouts  14.8 us (5%)
  between operations  14.5 us (5%)
    all_gather x1, waiting for transfers between devices, layer(): own_w = lax.all_gather(stacked, 'z', axis=1, tiled=True)  64.2 us
    reduce_scatter x1, waiting for transfers between devices, layer(): lax.psum_scatter(terms_chip.astype(jnp.bfloat16), 'z', scatter_dimension=...  55.1 us
    ppermute x3, waiting for transfers between devices, doubling_sum(): others = [lax.ppermute(m, axis, route) for m in mine]  37 us
    ppermute x7, waiting for transfers between devices, passed_along(): return lax.ppermute(block, axis, route)  20.3 us
    ppermute x3, waiting for transfers between devices, swapped_sum(): lax.ppermute(mine[:half], axis, [(0, 1), (1, 0)])  11.1 us
    ppermute x3, starting transfers between devices, swapped_sum(): lax.ppermute(mine[:half], axis, [(0, 1), (1, 0)])  9.47 us
    ppermute x3, waiting for transfers between devices, swapped_sum(): lax.ppermute(mine[half:], axis, [(0, 1), (1, 0)])  7.73 us
    ppermute x7, starting transfers between devices, passed_along(): return lax.ppermute(block, axis, route)  7.3 us
  transfers between devices with their start and end apart: 21, of which 15 were waited for; matrix products, arithmetic and copies ran while one was open for 10% of the time, Pallas kernels for 0%

profile of v4, /device:TPU:32, one launch (start us, length us, event | category | flops | bytes accessed | tf_op | source)
XLA Modules:
  0.0 310.2 jit_solution(13554181106108498343)
XLA Ops:
  7.2 2.0 pad_maximum_fusion.3
  9.5 64.2 %all-gather.2.cloned.1.call-done = bf16[2,576,2152]{2,1,0:T(8,128)(2,1)} async-done(((bf16[2,72,2152]{2,1,0:T(8,128)(2,1)}), bf16[2,576,2152]{2,1,0:T(8,128)(2,1)}) %all-gather.2.cloned.1.call-update) | async-done | bytes 4958224 | tf_op jit(solution)/shard_map/all_gather | solution.py:116
  74.5 2.3 collective-permute-start.7
  78.6 3.7 %collective-permute-done.7 = bf16[96,1152]{1,0:T(8,128)(2,1)S(1)} collective-permute-done((bf16[96,1152]{1,0:T(8,128)(2,1)S(1)}, bf16[96,1152]{1,0:T(8,128)(2,1)S(1)}, u32[]{:S(2)}, u32[]{:S(2)}) %collective-permute-start.7) | collective-permute-done | bytes 221216 | tf_op jit(solution)/shard_map/ppermute | solution.py:17
  82.3 2.3 collective-permute-start.8
  85.7 4.7 %collective-permute-done.8 = bf16[96,1152]{1,0:T(8,128)(2,1)S(1)} collective-permute-done((bf16[96,1152]{1,0:T(8,128)(2,1)S(1)}, bf16[96,1152]{1,0:T(8,128)(2,1)S(1)}, u32[]{:S(2)}, u32[]{:S(2)}) %collective-permute-start.8) | collective-permute-done | bytes 221216 | tf_op jit(solution)/shard_map/ppermute | solution.py:17
  90.4 1.2 collective-permute-start.9
  92.1 1.0 collective-permute-start.5
  93.9 5.5 %collective-permute-done.5 = bf16[96,1152]{1,0:T(8,128)(2,1)S(1)} collective-permute-done((bf16[96,1152]{1,0:T(8,128)(2,1)S(1)}, bf16[96,1152]{1,0:T(8,128)(2,1)S(1)}, u32[]{:S(2)}, u32[]{:S(2)}) %collective-permute-start.5) | collective-permute-done | bytes 221216 | tf_op jit(solution)/shard_map/ppermute | solution.py:17
  100.5 5.9 %collective-permute-done.6 = bf16[96,1152]{1,0:T(8,128)(2,1)S(1)} collective-permute-done((bf16[96,1152]{1,0:T(8,128)(2,1)S(1)}, bf16[96,1152]{1,0:T(8,128)(2,1)S(1)}, u32[]{:S(2)}, u32[]{:S(2)}) %collective-permute-start.6) | collective-permute-done | bytes 221216 | tf_op jit(solution)/shard_map/ppermute | solution.py:17
  109.7 2.7 fusion.9
  112.5 4.2 %multiply_convert_fusion = (bf16[192,2152]{1,0:T(8,128)(2,1)S(1)}, f32[192,2152]{1,0:T(8,128)}) fusion(f32[192,2152]{1,0:T(8,128)S(1)} %fusion.9, bf16[192,576]{0,1:T(8,128)(2,1)S(1)} %bitcast.123, bf16[2,576,2152]{2,1,0:T(8,128)(2,1)} %collective-permute-done), kind=kOutput, calls=%fused_computation.37 | convolution fusion | flops 480119808 | bytes 6859776 | tf_op jit(solution)/shard_map/dot_general | solution.py:127
  116.7 3.0 fusion.21
  119.8 1.0 fusion.22
  121.0 3.3 %collective-permute-start.1 = (bf16[96,1152]{1,0:T(8,128)(2,1)S(1)}, bf16[96,1152]{1,0:T(8,128)(2,1)S(1)}, u32[]{:S(2)}, u32[]{:S(2)}) collective-permute-start(bf16[96,1152]{1,0:T(8,128)(2,1)S(1)} %get-tuple-element.21), channel_id=1, source_target_pairs={{0,1},{1,0},{2,3},{3,2},{4,5},{5,4},{6,7},{7,6},{8,9},{9,8},{10,11... | collective-permute-start | bytes 663560 | tf_op jit(solution)/shard_map/ppermute | solution.py:29
  124.8 1.4 constant_dynamic-update-slice_fusion.8
  126.2 4.9 %collective-permute-done.1 = bf16[96,1152]{1,0:T(8,128)(2,1)S(1)} collective-permute-done((bf16[96,1152]{1,0:T(8,128)(2,1)S(1)}, bf16[96,1152]{1,0:T(8,128)(2,1)S(1)}, u32[]{:S(2)}, u32[]{:S(2)}) %collective-permute-start.1) | collective-permute-done | bytes 221216 | tf_op jit(solution)/shard_map/ppermute | solution.py:29
  131.1 4.3 %collective-permute-done.2 = bf16[96,1152]{1,0:T(8,128)(2,1)S(1)} collective-permute-done((bf16[96,1152]{1,0:T(8,128)(2,1)S(1)}, bf16[96,1152]{1,0:T(8,128)(2,1)S(1)}, u32[]{:S(2)}, u32[]{:S(2)}) %collective-permute-start.2) | collective-permute-done | bytes 221216 | tf_op jit(solution)/shard_map/ppermute | solution.py:30
  136.7 1.3 copy.19
  138.0 1.4 fusion.34
  139.4 5.3 %fusion.7 = bf16[192,1152]{1,0:T(8,128)(2,1)S(1)} fusion(bf16[1536,1152]{1,0:T(8,128)(2,1)} %constant_dynamic-update-slice_fusion.8, s32[1536]{0:T(1024)S(1)} %concatenate.51, s32[192]{0:T(256)S(1)} %iota_add_fusion, f32[192,1152]{1,0:T(8,128)S(1)} %copy.17, bf16[1,192,1152]{2,1,0:T(8,128)(2,1)S(1)} %copy-done, f32[192]{0:T(256)S(1)} %add_sqrt_fusion), kind=kOutput, calls=%fused_computation.21 | convolution fusion | flops 1362935808 | bytes 5316096 | tf_op jit(solution)/shard_map/dot_general | solution.py:153
  144.7 3.1 collective-permute-start.11
  148.4 6.3 %collective-permute-done.11 = bf16[96,1152]{1,0:T(8,128)(2,1)S(1)} collective-permute-done((bf16[96,1152]{1,0:T(8,128)(2,1)S(1)}, bf16[96,1152]{1,0:T(8,128)(2,1)S(1)}, u32[]{:S(2)}, u32[]{:S(2)}) %collective-permute-start.11) | collective-permute-done | bytes 221216 | tf_op jit(solution)/shard_map/ppermute | solution.py:29
  154.6 3.4 %collective-permute-done.12 = bf16[96,1152]{1,0:T(8,128)(2,1)S(1)} collective-permute-done((bf16[96,1152]{1,0:T(8,128)(2,1)S(1)}, bf16[96,1152]{1,0:T(8,128)(2,1)S(1)}, u32[]{:S(2)}, u32[]{:S(2)}) %collective-permute-start.12) | collective-permute-done | bytes 221216 | tf_op jit(solution)/shard_map/ppermute | solution.py:30
  158.4 1.2 fusion.57
  161.6 2.7 fusion.11
  164.4 3.5 %fusion.20 = bf16[192,2152]{1,0:T(8,128)(2,1)S(1)} fusion(f32[192,2152]{1,0:T(8,128)S(1)} %copy-done.7, f32[192,2152]{1,0:T(8,128)S(1)} %fusion.11, bf16[192,576]{0,1:T(8,128)(2,1)S(1)} %bitcast.126, bf16[2,576,2152]{2,1,0:T(8,128)(2,1)} %collective-permute-done), kind=kOutput, calls=%fused_computation.36 | convolution fusion | flops 484664832 | bytes 6859776 | tf_op jit(solution)/shard_map/rd,df->rf/dot_general | solution.py:162
  167.9 0.8 convolution_convert_fusion.1
  168.7 1.2 pad_maximum_fusion
  170.3 0.9 convolution_convert_fusion.2
  172.0 6.7 %collective-permute-done.15 = bf16[576,4304]{1,0:T(8,128)(2,1)} collective-permute-done((bf16[576,4304]{1,0:T(8,128)(2,1)S(1)}, bf16[576,4304]{1,0:T(8,128)(2,1)}, u32[]{:S(2)}, u32[]{:S(2)}) %collective-permute-start.15) | collective-permute-done | bytes 4958240 | tf_op jit(solution)/shard_map/ppermute | solution.py:21
  178.7 7.1 %add_convert_fusion = bf16[576,4304]{1,0:T(8,128)(2,1)} fusion(bf16[576,4304]{1,0:T(8,128)(2,1)} %collective-permute-done.15, bf16[576,2152]{1,0:T(8,128)(2,1)S(1)} %convolution_convert_fusion.2, bf16[576,2152]{1,0:T(8,128)(2,1)S(1)} %convolution_convert_fusion.3), kind=kLoop, calls=%fused_computation | loop fusion | flops 17353728 | bytes 14874624 | tf_op jit(solution)/shard_map/convert_element_type | solution.py:201
  185.8 2.7 fusion.23
  188.6 2.7 fusion.24
  191.4 3.1 collective-permute-start.13
  195.1 55.1 %reduce-scatter.2.cloned.1.call-done = bf16[72,4304]{1,0:T(8,128)(2,1)} async-done(((bf16[576,4304]{1,0:T(8,128)(2,1)}), bf16[72,4304]{1,0:T(8,128)(2,1)}) %reduce-scatter.2.cloned.1.call-update) | async-done | bytes 619792 | tf_op jit(solution)/shard_map/reduce_scatter | solution.py:200
  250.1 1.5 collective-permute-start.16
  252.2 1.0 copy.22
  253.2 13.0 %collective-permute-done.16 = bf16[72,4304]{1,0:T(8,128)(2,1)} collective-permute-done((bf16[72,4304]{1,0:T(8,128)(2,1)}, bf16[72,4304]{1,0:T(8,128)(2,1)}, u32[]{:S(2)}, u32[]{:S(2)}) %collective-permute-start.16) | collective-permute-done | bytes 619808 | tf_op jit(solution)/shard_map/ppermute | solution.py:43
  266.2 1.4 add_convert_fusion.2
  267.7 1.6 collective-permute-start.17
  270.1 12.6 %collective-permute-done.17 = bf16[72,4304]{1,0:T(8,128)(2,1)} collective-permute-done((bf16[72,4304]{1,0:T(8,128)(2,1)S(1)}, bf16[72,4304]{1,0:T(8,128)(2,1)}, u32[]{:S(2)}, u32[]{:S(2)}) %collective-permute-start.17) | collective-permute-done | bytes 619808 | tf_op jit(solution)/shard_map/ppermute | solution.py:43
  282.8 2.0 add_convert_fusion.1
  284.8 3.0 collective-permute-start.18
  288.2 1.2 fusion.32
  289.4 11.3 %collective-permute-done.18 = bf16[72,4304]{1,0:T(8,128)(2,1)} collective-permute-done((bf16[72,4304]{1,0:T(8,128)(2,1)}, bf16[72,4304]{1,0:T(8,128)(2,1)}, u32[]{:S(2)}, u32[]{:S(2)}) %collective-permute-start.18) | collective-permute-done | bytes 619808 | tf_op jit(solution)/shard_map/ppermute | solution.py:43
  300.7 1.4 convert_add_fusion
  302.1 1.2 slice_bitcast_fusion.22
  (95 shorter events, 18.1 us)
Async XLA Ops:
  7.2 2.2 copy-start.5
  7.2 69.6 %copy-start.6 = (f32[1152]{0:T(1024)S(1)}, f32[1152]{0:T(1024)}, u32[]{:S(2)}) copy-start(f32[1152]{0:T(1024)} %param.6) | copy-start | bytes 13828
  7.2 69.7 %copy-start = (bf16[1,192,1152]{2,1,0:T(8,128)(2,1)S(1)}, bf16[1,192,1152]{2,1,0:T(8,128)(2,1)}, u32[]{:S(2)}) copy-start(bf16[1,192,1152]{2,1,0:T(8,128)(2,1)} %param.5) | copy-start | bytes 1327108
  7.2 66.5 %all-gather.2.cloned.1.call-start = ((), (), s32[]{:S(2)}) async-start(), calls=%async_computation.1 | async-start | bytes 5640192 | tf_op jit(solution)/shard_map/all_gather | solution.py:116
  9.3 240.8 %reduce-scatter.2.cloned.1.call-start = ((), (), s32[]{:S(2)}) async-start(), calls=%async_computation.2 | async-start | bytes 5640192 | tf_op jit(solution)/shard_map/reduce_scatter | solution.py:200
  73.7 38.8 %collective-permute-start = (bf16[2,576,2152]{2,1,0:T(8,128)(2,1)}, bf16[2,576,2152]{2,1,0:T(8,128)(2,1)}, u32[]{:S(2)}, u32[]{:S(2)}) collective-permute-start(bf16[2,576,2152]{2,1,0:T(8,128)(2,1)} %all-gather.2.cloned.1.call-done), channel_id=1, source_target_pairs={{0,2},{2,0},{1,3},{3,1},{4,6},{6,4},{5,7},{7,5},{8,10},{10,8},{9,1... | collective-permute-start | bytes 14874632 | tf_op jit(solution)/shard_map/ppermute | solution.py:21
  74.5 7.8 %collective-permute-start.7 = (bf16[96,1152]{1,0:T(8,128)(2,1)S(1)}, bf16[96,1152]{1,0:T(8,128)(2,1)S(1)}, u32[]{:S(2)}, u32[]{:S(2)}) collective-permute-start(bf16[96,1152]{1,0:T(8,128)(2,1)S(1)} %get-tuple-element.6), channel_id=1, source_target_pairs={{4,0},{8,4},{12,8},{16,12},{20,16},{24,20},{28,24},{0,28},{5,1},{9... | collective-permute-start | bytes 663560 | tf_op jit(solution)/shard_map/ppermute | solution.py:17
  76.8 7.8 %collective-permute-start.3 = (bf16[96,1152]{1,0:T(8,128)(2,1)S(1)}, bf16[96,1152]{1,0:T(8,128)(2,1)S(1)}, u32[]{:S(2)}, u32[]{:S(2)}) collective-permute-start(bf16[96,1152]{1,0:T(8,128)(2,1)S(1)} %get-tuple-element.6), channel_id=1, source_target_pairs={{28,0},{0,4},{4,8},{8,12},{12,16},{16,20},{20,24},{24,28},{29,1},{... | collective-permute-start | bytes 663560 | tf_op jit(solution)/shard_map/ppermute | solution.py:17
  82.3 8.1 %collective-permute-start.8 = (bf16[96,1152]{1,0:T(8,128)(2,1)S(1)}, bf16[96,1152]{1,0:T(8,128)(2,1)S(1)}, u32[]{:S(2)}, u32[]{:S(2)}) collective-permute-start(bf16[96,1152]{1,0:T(8,128)(2,1)S(1)} %collective-permute-done.7), channel_id=1, source_target_pairs={{4,0},{8,4},{12,8},{16,12},{20,16},{24,20},{28,24},{0,28},{5,1},{9... | collective-permute-start | bytes 663560 | tf_op jit(solution)/shard_map/ppermute | solution.py:17
  84.6 7.5 %collective-permute-start.4 = (bf16[96,1152]{1,0:T(8,128)(2,1)S(1)}, bf16[96,1152]{1,0:T(8,128)(2,1)S(1)}, u32[]{:S(2)}, u32[]{:S(2)}) collective-permute-start(bf16[96,1152]{1,0:T(8,128)(2,1)S(1)} %collective-permute-done.3), channel_id=1, source_target_pairs={{28,0},{0,4},{4,8},{8,12},{12,16},{16,20},{20,24},{24,28},{29,1},{... | collective-permute-start | bytes 663560 | tf_op jit(solution)/shard_map/ppermute | solution.py:17
  90.4 18.4 %collective-permute-start.9 = (bf16[96,1152]{1,0:T(8,128)(2,1)S(1)}, bf16[96,1152]{1,0:T(8,128)(2,1)S(1)}, u32[]{:S(2)}, u32[]{:S(2)}) collective-permute-start(bf16[96,1152]{1,0:T(8,128)(2,1)S(1)} %collective-permute-done.8), channel_id=1, source_target_pairs={{4,0},{8,4},{12,8},{16,12},{20,16},{24,20},{28,24},{0,28},{5,1},{9... | collective-permute-start | bytes 663560 | tf_op jit(solution)/shard_map/ppermute | solution.py:17
  92.1 7.3 %collective-permute-start.5 = (bf16[96,1152]{1,0:T(8,128)(2,1)S(1)}, bf16[96,1152]{1,0:T(8,128)(2,1)S(1)}, u32[]{:S(2)}, u32[]{:S(2)}) collective-permute-start(bf16[96,1152]{1,0:T(8,128)(2,1)S(1)} %collective-permute-done.4), channel_id=1, source_target_pairs={{28,0},{0,4},{4,8},{8,12},{12,16},{16,20},{20,24},{24,28},{29,1},{... | collective-permute-start | bytes 663560 | tf_op jit(solution)/shard_map/ppermute | solution.py:17
  99.5 7.0 %collective-permute-start.6 = (bf16[96,1152]{1,0:T(8,128)(2,1)S(1)}, bf16[96,1152]{1,0:T(8,128)(2,1)S(1)}, u32[]{:S(2)}, u32[]{:S(2)}) collective-permute-start(bf16[96,1152]{1,0:T(8,128)(2,1)S(1)} %collective-permute-done.5), channel_id=1, source_target_pairs={{28,0},{0,4},{4,8},{8,12},{12,16},{16,20},{20,24},{24,28},{29,1},{... | collective-permute-start | bytes 663560 | tf_op jit(solution)/shard_map/ppermute | solution.py:17
  109.6 15.2 %collective-permute-start.10 = (bf16[768,1152]{1,0:T(8,128)(2,1)}, bf16[768,1152]{1,0:T(8,128)(2,1)S(1)}, u32[]{:S(2)}, u32[]{:S(2)}) collective-permute-start(bf16[768,1152]{1,0:T(8,128)(2,1)} %get-tuple-element.25), channel_id=1, source_target_pairs={{0,2},{2,0},{1,3},{3,1},{4,6},{6,4},{5,7},{7,5},{8,10},{10,8},{9,1... | collective-permute-start | bytes 5308424 | tf_op jit(solution)/shard_map/ppermute | solution.py:21
  109.7 10.0 %slice-start = ((s8[5013504]{0:T(1024)(128)(4,1)}), s8[4194304]{0:T(1024)(128)(4,1)S(1)}, s32[]{:S(2)}) async-start(s8[5013504]{0:T(1024)(128)(4,1)} %bitcast.111), calls=%async_computation.3 | async-start | bytes 8388608
  112.5 7.3 %slice-start.1 = ((s8[5013504]{0:T(1024)(128)(4,1)}), s8[819200]{0:T(1024)(128)(4,1)S(1)}, s32[]{:S(2)}) async-start(s8[5013504]{0:T(1024)(128)(4,1)} %bitcast.111), calls=%async_computation.4 | async-start | bytes 1638400
  116.7 3.0 copy-start.2
  121.0 10.1 %collective-permute-start.1 = (bf16[96,1152]{1,0:T(8,128)(2,1)S(1)}, bf16[96,1152]{1,0:T(8,128)(2,1)S(1)}, u32[]{:S(2)}, u32[]{:S(2)}) collective-permute-start(bf16[96,1152]{1,0:T(8,128)(2,1)S(1)} %get-tuple-element.21), channel_id=1, source_target_pairs={{0,1},{1,0},{2,3},{3,2},{4,5},{5,4},{6,7},{7,6},{8,9},{9,8},{10,11... | collective-permute-start | bytes 663560 | tf_op jit(solution)/shard_map/ppermute | solution.py:29
  124.3 11.1 %collective-permute-start.2 = (bf16[96,1152]{1,0:T(8,128)(2,1)S(1)}, bf16[96,1152]{1,0:T(8,128)(2,1)S(1)}, u32[]{:S(2)}, u32[]{:S(2)}) collective-permute-start(bf16[96,1152]{1,0:T(8,128)(2,1)S(1)} %get-tuple-element.22), channel_id=1, source_target_pairs={{0,1},{1,0},{2,3},{3,2},{4,5},{5,4},{6,7},{7,6},{8,9},{9,8},{10,11... | collective-permute-start | bytes 663560 | tf_op jit(solution)/shard_map/ppermute | solution.py:30
  144.7 9.9 %collective-permute-start.11 = (bf16[96,1152]{1,0:T(8,128)(2,1)S(1)}, bf16[96,1152]{1,0:T(8,128)(2,1)S(1)}, u32[]{:S(2)}, u32[]{:S(2)}) collective-permute-start(bf16[96,1152]{1,0:T(8,128)(2,1)S(1)} %get-tuple-element.23), channel_id=1, source_target_pairs={{0,1},{1,0},{2,3},{3,2},{4,5},{5,4},{6,7},{7,6},{8,9},{9,8},{10,11... | collective-permute-start | bytes 663560 | tf_op jit(solution)/shard_map/ppermute | solution.py:29
  147.8 10.2 %collective-permute-start.12 = (bf16[96,1152]{1,0:T(8,128)(2,1)S(1)}, bf16[96,1152]{1,0:T(8,128)(2,1)S(1)}, u32[]{:S(2)}, u32[]{:S(2)}) collective-permute-start(bf16[96,1152]{1,0:T(8,128)(2,1)S(1)} %get-tuple-element.24), channel_id=1, source_target_pairs={{0,1},{1,0},{2,3},{3,2},{4,5},{5,4},{6,7},{7,6},{8,9},{9,8},{10,11... | collective-permute-start | bytes 663560 | tf_op jit(solution)/shard_map/ppermute | solution.py:30
  159.6 1.1 copy-start.3
  161.6 2.7 copy-start.7
  170.0 8.8 %collective-permute-start.15 = (bf16[576,4304]{1,0:T(8,128)(2,1)S(1)}, bf16[576,4304]{1,0:T(8,128)(2,1)}, u32[]{:S(2)}, u32[]{:S(2)}) collective-permute-start(bf16[576,4304]{1,0:T(8,128)(2,1)S(1)} %pad_maximum_fusion), channel_id=1, source_target_pairs={{0,2},{2,0},{1,3},{3,1},{4,6},{6,4},{5,7},{7,5},{8,10},{10,8},{9,1... | collective-permute-start | bytes 14874632 | tf_op jit(solution)/shard_map/ppermute | solution.py:21
  191.4 60.2 %collective-permute-start.13 = (bf16[96,1152]{1,0:T(8,128)(2,1)S(1)}, bf16[96,1152]{1,0:T(8,128)(2,1)S(1)}, u32[]{:S(2)}, u32[]{:S(2)}) collective-permute-start(bf16[96,1152]{1,0:T(8,128)(2,1)S(1)} %get-tuple-element.19), channel_id=1, source_target_pairs={{0,1},{1,0},{2,3},{3,2},{4,5},{5,4},{6,7},{7,6},{8,9},{9,8},{10,11... | collective-permute-start | bytes 663560 | tf_op jit(solution)/shard_map/ppermute | solution.py:29
  194.5 57.1 %collective-permute-start.14 = (bf16[96,1152]{1,0:T(8,128)(2,1)S(1)}, bf16[96,1152]{1,0:T(8,128)(2,1)S(1)}, u32[]{:S(2)}, u32[]{:S(2)}) collective-permute-start(bf16[96,1152]{1,0:T(8,128)(2,1)S(1)} %get-tuple-element.20), channel_id=1, source_target_pairs={{0,1},{1,0},{2,3},{3,2},{4,5},{5,4},{6,7},{7,6},{8,9},{9,8},{10,11... | collective-permute-start | bytes 663560 | tf_op jit(solution)/shard_map/ppermute | solution.py:30
  250.1 16.1 %collective-permute-start.16 = (bf16[72,4304]{1,0:T(8,128)(2,1)}, bf16[72,4304]{1,0:T(8,128)(2,1)}, u32[]{:S(2)}, u32[]{:S(2)}) collective-permute-start(bf16[72,4304]{1,0:T(8,128)(2,1)} %reduce-scatter.2.cloned.1.call-done), channel_id=1, source_target_pairs={{0,32},{32,0},{64,96},{96,64},{128,160},{160,128},{192,224},{224,1... | collective-permute-start | bytes 1859336 | tf_op jit(solution)/shard_map/ppermute | solution.py:43
  253.2 16.0 %copy-start.4 = (f32[192,576]{0,1:T(8,128)S(1)}, f32[192,576]{0,1:T(8,128)}, u32[]{:S(2)}) copy-start(f32[192,576]{0,1:T(8,128)} %copy.22) | copy-start | bytes 1327108
  267.7 15.1 %collective-permute-start.17 = (bf16[72,4304]{1,0:T(8,128)(2,1)S(1)}, bf16[72,4304]{1,0:T(8,128)(2,1)}, u32[]{:S(2)}, u32[]{:S(2)}) collective-permute-start(bf16[72,4304]{1,0:T(8,128)(2,1)S(1)} %add_convert_fusion.2), channel_id=1, source_target_pairs={{0,64},{32,96},{64,0},{96,32},{128,192},{160,224},{192,128},{224,1... | collective-permute-start | bytes 1859336 | tf_op jit(solution)/shard_map/ppermute | solution.py:43
  270.1 18.0 %copy-start.1 = (f32[192,1152]{1,0:T(8,128)S(1)}, f32[192,1152]{1,0:T(8,128)}, u32[]{:S(2)}) copy-start(f32[192,1152]{1,0:T(8,128)} %get-tuple-element.4) | copy-start | bytes 2654212
  284.8 15.9 %collective-permute-start.18 = (bf16[72,4304]{1,0:T(8,128)(2,1)}, bf16[72,4304]{1,0:T(8,128)(2,1)}, u32[]{:S(2)}, u32[]{:S(2)}) collective-permute-start(bf16[72,4304]{1,0:T(8,128)(2,1)} %add_convert_fusion.1), channel_id=1, source_target_pairs={{0,128},{32,160},{64,192},{96,224},{128,0},{160,32},{192,64},{224,... | collective-permute-start | bytes 1859336 | tf_op jit(solution)/shard_map/ppermute | solution.py:43
Sparse Core Ops, SparseCore 0:
  10.4 63.2 all-gather.1
  186.0 64.1 reduce-scatter.1
